TPU v7x, 32 devices: a whole 2x2x4 slice. The times are simulated.
32 devices in a mesh: mem: 16 (over z, x, core), gy: 2 (over y).
Axes of the slice: x: 2, y: 2, z: 4, core: 2. Of those that a mesh axis runs over, the one named last changes fastest.
Arguments:
- state: bfloat16 [64, 2, 512, 256], P('mem', None, None, 'gy'), may hold values from -6 to 6
- obs_index: int32 [16, 2, 256], P('mem', 'gy'), may hold values from 0 to 8191
- obs_count: int32 [16, 2], P('mem', 'gy'), may hold values from 1 to 256, as said below
- obs_value: float32 [16, 2, 256], P('mem', 'gy'), may hold values from -6 to 6
- obs_var: float32 [16, 2, 256], P('mem', 'gy'), may hold values from 0.1 to 1
- radius: int32 [16, 2], P('mem', 'gy'), may hold values from 8 to 16
Outputs:
- analysis: bfloat16 [64, 2, 512, 256], P('mem', None, None, 'gy')
Inputs may be any that keep to these rules, and one draw needn't show every extreme that they name: `obs_count`: Tiles' counts are skewed: most tiles have few live slots, some many, and in every draw some tile has all 256 slots live.
All inputs are finite; a program needn't handle non-finite values.
Results may differ from a plain program's by a relative error of at most 0.0028.
The roundings to bfloat16 on the way count: a program that leaves them out, or rounds other values in their place, can miss the bound.
Values may be sent and summed in bfloat16 or wider, within the bound.
No kernel may reach another device: no remote copies, remote signals or barrier semaphores. Data moves between devices by JAX's collectives and lax.ppermute only.
A program may use at most 64 MiB of HBM per device.

v0:
```python
import functools
import math

import jax
import jax.numpy as jnp
from jax import lax
from jax.experimental import pallas as pl
from jax.experimental.pallas import tpu as pltpu
from jax.sharding import PartitionSpec as P

BLK = 16
NSI = 10
f32 = jnp.float32
bf16 = jnp.bfloat16
META = 8


def dot(a, b):
    return lax.dot_general(a, b, (((1,), (0,)), ((), ())), preferred_element_type=f32)


def dot_t(a, b):
    return lax.dot_general(a, b, (((1,), (1,)), ((), ())), preferred_element_type=f32)


def split3(x):
    high = x.astype(bf16)
    rest = x - high.astype(f32)
    mid = rest.astype(bf16)
    low = (rest - mid.astype(f32)).astype(bf16)
    return high, mid, low


def gather_kernel(x_ref, idx_ref, ens_ref):
    members, cells, rows = x_ref.shape
    slots = idx_ref.shape[1]
    idx = idx_ref[...]
    row = lax.rem(idx, rows)
    cell = lax.div(idx, rows)
    pick_row = jnp.where(lax.broadcasted_iota(jnp.int32, (rows, slots), 0) == row, 1.0, 0.0).astype(bf16)
    pick_cell = lax.broadcasted_iota(jnp.int32, (cells, slots), 0) == cell
    for first in range(0, members, 8):
        x = x_ref[first : first + 8].reshape(8 * cells, rows)
        found = dot(x, pick_row).reshape(8, cells, slots)
        ens_ref[first : first + 8, :] = jnp.sum(jnp.where(pick_cell[None], found, 0.0), axis=1)


def gather_call(x, obs_slots):
    members, cells, rows = x.shape
    slots = obs_slots.shape[0]
    group = min(members, 16)
    return pl.pallas_call(
        gather_kernel,
        grid=(members // group,),
        in_specs=[
            pl.BlockSpec((group, cells, rows), lambda i: (i, 0, 0)),
            pl.BlockSpec((1, slots), lambda i: (0, 0)),
        ],
        out_specs=pl.BlockSpec((group, slots), lambda i: (i, 0)),
        out_shape=jax.ShapeDtypeStruct((members, slots), f32),
        name="gather",
    )(x, obs_slots[None])


def recursion_product(a, b, left):
    ah, am, al = a
    bh, bm, bl = b
    return dot(
        jnp.concatenate([ah, am, jnp.where(left, al, ah)], axis=1),
        jnp.concatenate([bh, bm, bh, bm, bh, bl], axis=0),
    )


def transform_kernel(num_y, counts, scal_ref, *refs):
    count_c, count_r, cols, rows = counts
    ens_refs = refs[: 3 * num_y]
    meta_refs = refs[3 * num_y : 4 * num_y]
    out_ref, lhs_ref, gram_ref, up_ref, low_ref = refs[4 * num_y :]
    members, slots = ens_refs[0].shape
    wide = 2 * members
    odd_x = scal_ref[0] == 1
    odd_y = scal_ref[1] == 1
    reach = scal_ref[2].astype(f32)
    reach_sq = reach * reach

    def tile(y, which):
        own, pair, other = ens_refs[3 * y : 3 * y + 3]
        if which == 0:
            return own[...].astype(f32), meta_refs[y][0]
        pair_first = odd_x if which < 0 else jnp.logical_not(odd_x)
        ens = jnp.where(pair_first, pair[...].astype(f32), other[...].astype(f32))
        meta = jnp.where(pair_first, meta_refs[y][1], meta_refs[y][2])
        return ens, meta

    def prepare(y, which):
        ens, meta = tile(y, which)
        centre = jnp.sum(ens, axis=0, keepdims=True) * (1.0 / members)
        spread = ens - centre
        innovation = meta[0:1] - centre
        sh, sm, sl = split3(spread)
        line = lax.broadcasted_iota(jnp.int32, (members, slots), 0)
        ih, im, il = (part.astype(f32) for part in split3(innovation))
        extra = jnp.where(line == 0, ih, jnp.where(line == 1, im, jnp.where(line == 2, il, 0.0))).astype(bf16)
        return spread, meta, jnp.concatenate([sh, sm, sl, extra], axis=0)

    def local_weight(meta, dx, dy, block_c, block_r):
        gap_c = dx * cols + meta[2:3] - (block_c * float(BLK) + (BLK - 1) / 2.0)
        gap_r = dy * float(rows) + meta[3:4] - (block_r * float(BLK) + (BLK - 1) / 2.0)
        taper = jnp.maximum(1.0 - (gap_c * gap_c + gap_r * gap_r) / reach_sq, 0.0)
        return taper * taper * meta[1:2]

    def put(part, total, column, rho, spread):
        weighted = rho * spread
        for level, piece in enumerate(split3(weighted)):
            start = level * total + part * members
            lhs_ref[start : start + members, column : column + slots] = piece

    own_tiles = [prepare(y, 0) for y in range(num_y)]
    lines = lax.broadcasted_iota(jnp.int32, (count_r, slots), 0).astype(f32)
    for a in range(count_c):
        sides = [0] + ([-1] if a == 0 else []) + ([1] if a == count_c - 1 else [])
        tiles = [[own_tiles[y] if side == 0 else prepare(y, side) for side in sides] for y in range(num_y)]
        total = count_r * members
        for at, (side, (spread, meta, rhs)) in enumerate(zip(sides, tiles[0])):
            rho = local_weight(meta, float(side), 0.0, float(a), lines)
            for r in range(count_r):
                put(r, total, at * slots, rho[r : r + 1], spread)
        width = len(sides) * slots
        rhs = jnp.concatenate([t[2] for t in tiles[0]], axis=1)
        found = dot_t(lhs_ref[: 3 * total, :width], rhs)
        found = found[:total] + found[total : 2 * total] + found[2 * total :]
        gram_ref[a * count_r : (a + 1) * count_r] = found.reshape(count_r, members, 4 * members)
        for y in range(1, num_y):
            above = jnp.logical_not(odd_y) if y == 1 else odd_y
            dy = jnp.where(above, 1.0, -1.0)
            edge = jnp.where(above, count_r - 1, 0)
            for at, (side, (spread, meta, rhs)) in enumerate(zip(sides, tiles[y])):
                rho = local_weight(meta, float(side), dy, float(a), edge.astype(f32))
                put(0, members, at * slots, rho, spread)
            rhs = jnp.concatenate([t[2] for t in tiles[y]], axis=1)
            found = dot_t(lhs_ref[: 3 * members, :width], rhs)
            found = found[:members] + found[members : 2 * members] + found[2 * members :]
            gram_ref[a * count_r + edge] += found

    blocks = count_c * count_r
    line = lax.broadcasted_iota(jnp.int32, (members, wide), 0)
    lane = lax.broadcasted_iota(jnp.int32, (members, wide), 1)
    left = lane < members
    half = jnp.where(lane == line, 1.0, 0.0)
    eye = jnp.where(lane == line + members, 1.0, half)

    def keep(ref, b, value):
        for part, piece in enumerate(split3(value)):
            ref[b, part] = piece

    def held(ref, b):
        return ref[b, 0], ref[b, 1], ref[b, 2]

    scales = []
    drives = []
    starts = []
    for b in range(blocks):
        found = gram_ref[b]
        high, tail = found[:, :wide], found[:, wide:]
        once = high + jnp.where(left, tail, 0.0)
        system = (members - 1.0) * eye + once + pltpu.roll(once, members, 1)
        drive = jnp.sum(jnp.where(left, 0.0, tail), axis=1, keepdims=True)
        drives.append(jnp.sum(drive * eye, axis=0, keepdims=True))
        scale = jnp.sum(jnp.sum(system * half, axis=1, keepdims=True), axis=0, keepdims=True)
        scales.append(scale)
        starts.append(system / scale)
    for b in range(blocks):
        factor = 1.5 * eye - 0.5 * starts[b]
        keep(low_ref, b, factor)
        keep(up_ref, b, recursion_product(split3(starts[b]), split3(factor), left))

    def sweep(_, carry):
        factors = []
        for b in range(blocks):
            product = recursion_product(held(low_ref, b), held(up_ref, b), left)
            factors.append(split3(1.5 * eye - 0.5 * product))
        for b in range(blocks):
            upper = recursion_product(held(up_ref, b), factors[b], left)
            lower = recursion_product(factors[b], held(low_ref, b), left)
            keep(up_ref, b, upper)
            keep(low_ref, b, lower)
        return carry

    lax.fori_loop(0, NSI - 1, sweep, 0)

    mixed = []
    for b in range(blocks):
        lh, lm, ll = held(low_ref, b)
        lower = lh.astype(f32) + lm.astype(f32) + ll.astype(f32)
        inv_root = lower * lax.rsqrt(scales[b])
        first = jnp.sum(jnp.where(left, inv_root * drives[b], 0.0), axis=1, keepdims=True)
        shift = jnp.sum(inv_root * first, axis=0, keepdims=True)
        transform = math.sqrt(members - 1.0) * inv_root + shift
        mean = jnp.sum(jnp.where(left, transform, 0.0), axis=1, keepdims=True) * (1.0 / members)
        mixed.append(1.0 / members + transform - mean)
    for a in range(count_c):
        for r in range(0, count_r, 2):
            b = a * count_r + r
            both = jnp.where(left, mixed[b], mixed[b + 1])
            out_ref[a, :, r * members : (r + 2) * members] = both.astype(bf16)


def transform_call(scalars, ens, meta, cols, rows):
    num_y = len(meta)
    members, slots = ens[0].shape
    count_c, count_r = cols // BLK, rows // BLK
    blocks = count_c * count_r
    vmem = pl.BlockSpec(memory_space=pltpu.VMEM)
    return pl.pallas_call(
        functools.partial(transform_kernel, num_y, (count_c, count_r, cols, rows)),
        in_specs=[pl.BlockSpec(memory_space=pltpu.SMEM)] + [vmem] * (4 * num_y),
        out_specs=vmem,
        out_shape=jax.ShapeDtypeStruct((count_c, members, count_r * members), bf16),
        scratch_shapes=[
            pltpu.VMEM((3 * count_r * members, 2 * slots), bf16),
            pltpu.VMEM((blocks, members, 4 * members), f32),
            pltpu.VMEM((blocks, 3, members, 2 * members), bf16),
            pltpu.VMEM((blocks, 3, members, 2 * members), bf16),
        ],
        name="transform",
    )(scalars, *ens, *meta)


def mix_kernel(count_c, count_r, cols, mix_ref, x_ref, out_ref, in32_ref, out32_ref):
    members, cells, rows = x_ref.shape
    for k in range(0, members, 8):
        in32_ref[k * cells : (k + 8) * cells] = x_ref[k : k + 8].reshape(8 * cells, rows).astype(f32)
    lane_block = lax.broadcasted_iota(jnp.int32, (members, rows), 1) // BLK
    masks = [(lane_block == r) for r in range(count_r)]
    zero = jnp.zeros((members, rows), bf16)
    for cell in range(0, cells, 2):
        a = (cell % cols) // BLK
        pieces = []
        for one in (cell, cell + 1):
            x = in32_ref[pl.ds(one, members, stride=cells), :].astype(bf16)
            pieces.append(jnp.concatenate([jnp.where(mask, x, zero) for mask in masks], axis=0))
        found = dot(mix_ref[a], jnp.concatenate(pieces, axis=1))
        for at in range(2):
            out32_ref[pl.ds(cell + at, members, stride=cells), :] = found[:, at * rows : (at + 1) * rows]
    for k in range(0, members, 8):
        out_ref[k : k + 8] = out32_ref[k * cells : (k + 8) * cells].astype(bf16).reshape(8, cells, rows)


def mix_call(mixing, x, cols):
    members, cells, rows = x.shape
    count_c, count_r = cols // BLK, rows // BLK
    vmem = pl.BlockSpec(memory_space=pltpu.VMEM)
    return pl.pallas_call(
        functools.partial(mix_kernel, count_c, count_r, cols),
        in_specs=[vmem, vmem],
        out_specs=vmem,
        out_shape=jax.ShapeDtypeStruct(x.shape, bf16),
        scratch_shapes=[pltpu.VMEM((members * cells, rows), f32)] * 2,
        name="mix",
    )(mixing, x)


def swap_pairs(count, first):
    pairs = []
    for i in range(first, count - 1, 2):
        pairs += [(i, i + 1), (i + 1, i)]
    return pairs


def local(state, obs_index, obs_count, obs_value, obs_var, radius):
    n_x = lax.axis_size("mem")
    n_y = lax.axis_size("gy")
    held, levels, all_cols, rows = state.shape
    cols = all_cols // n_x
    members = held * n_x
    obs_slots = obs_index[0, 0]
    slots = obs_slots.shape[0]

    def swap_x(value, first):
        return lax.ppermute(value, "mem", swap_pairs(n_x, first))

    def swap_y(value, first):
        return lax.ppermute(value, "gy", swap_pairs(n_y, first))

    def swap_xy(value, first_x, first_y):
        pairs = [
            (sx * n_y + sy, dx * n_y + dy)
            for sx, dx in swap_pairs(n_x, first_x)
            for sy, dy in swap_pairs(n_y, first_y)
        ]
        return lax.ppermute(value, ("mem", "gy"), pairs)

    y_steps = [first for first in (0, 1) if swap_pairs(n_y, first)]

    live = jnp.arange(slots, dtype=jnp.int32) < obs_count[0, 0]
    weight = jnp.where(live, 1.0 / obs_var[0, 0], 0.0)
    col_pos = (obs_slots // rows % cols).astype(f32)
    row_pos = (obs_slots % rows).astype(f32)
    blank = jnp.zeros((META - 4, slots), f32)
    meta = jnp.concatenate([jnp.stack([obs_value[0, 0], weight, col_pos, row_pos]), blank], axis=0)
    meta_row = jnp.stack([meta, swap_x(meta, 0), swap_x(meta, 1)])
    meta_rows = [meta_row] + [swap_y(meta_row, first) for first in y_steps]

    chunks = state.reshape(held, levels, n_x, cols, rows).transpose(2, 0, 1, 3, 4)
    tile = lax.all_to_all(chunks, "mem", split_axis=0, concat_axis=0, tiled=True)
    tile = tile.reshape(members, levels * cols, rows)

    own = gather_call(tile, obs_slots).astype(bf16)
    pair = swap_x(own, 0)
    ens = [own, pair, swap_x(own, 1)]
    both = jnp.stack([own, pair])
    for first in y_steps:
        beside = swap_y(both, first)
        ens += [beside[0], beside[1], swap_xy(own, 1, first)]

    scalars = jnp.stack(
        [lax.axis_index("mem") % 2, lax.axis_index("gy") % 2, radius[0, 0]]
    ).astype(jnp.int32)
    mixing = transform_call(scalars, ens, meta_rows, cols, rows)
    analysed = mix_call(mixing, tile, cols)

    analysed = analysed.reshape(n_x, held, levels, cols, rows)
    back = lax.all_to_all(analysed, "mem", split_axis=0, concat_axis=0, tiled=True)
    return back.transpose(1, 2, 0, 3, 4).reshape(state.shape)


def solution(mesh):
    in_specs = (
        P("mem", None, None, "gy"),
        P("mem", "gy", None),
        P("mem", "gy"),
        P("mem", "gy", None),
        P("mem", "gy", None),
        P("mem", "gy"),
    )
    out_specs = P("mem", None, None, "gy")
    return jax.shard_map(local, mesh=mesh, in_specs=in_specs, out_specs=out_specs, check_vma=False)
```

profile of v0, /device:TPU:1, one launch (start us, length us, event | category | flops | bytes accessed | tf_op | source)
XLA Modules:
  0.0 105.0 jit_solution(17483820199834794085)
XLA Ops:
  0.0 2.3 %copy.10 = bf16[4,2,16,32,128]{4,3,1,0,2:T(8,128)(2,1)} copy(bf16[4,2,16,32,128]{4,3,2,1,0:T(8,128)(2,1)} %bitcast.35) | data formatting | bytes 2097152 | tf_op jit(solution)/shard_map/reshape | solution.py:304
  2.3 7.3 %all-to-all-start = ((bf16[16,4,2,32,128]{4,3,2,1,0:T(8,128)(2,1)}), bf16[16,4,2,32,128]{4,3,2,1,0:T(8,128)(2,1)S(1)}, u32[]{:S(2)}, u32[]{:S(2)}) async-start(bf16[16,4,2,32,128]{4,3,2,1,0:T(8,128)(2,1)} %bitcast.28), calls=%async_computation | async-start | bytes 2097152 | tf_op jit(solution)/shard_map/all_to_all | solution.py:305
  10.3 0.0 copy-start.10
  10.3 0.7 copy-done.10
  11.0 0.0 copy-start.8
  11.0 0.7 copy-done.8
  11.7 0.0 copy-start.9
  11.7 0.7 copy-done.9
  12.4 3.5 %collective-permute-start.5 = (f32[8,256]{1,0:T(8,128)S(1)}, f32[8,256]{1,0:T(8,128)S(1)}, u32[]{:S(2)}, u32[]{:S(2)}) collective-permute-start(f32[8,256]{1,0:T(8,128)S(1)} %concatenate.3), channel_id=1, source_target_pairs={{2,4},{4,2},{6,8},{8,6},{10,12},{12,10},{14,16},{16,14},{18,20},{2... | collective-permute-start | bytes 24584 | tf_op jit(solution)/shard_map/ppermute | solution.py:280
  16.0 0.1 collective-permute-start.4
  16.7 0.7 pad_add_fusion.scal_ref
  17.4 15.5 %all-to-all-done = bf16[16,4,2,32,128]{4,3,2,1,0:T(8,128)(2,1)S(1)} async-done(((bf16[16,4,2,32,128]{4,3,2,1,0:T(8,128)(2,1)}), bf16[16,4,2,32,128]{4,3,2,1,0:T(8,128)(2,1)S(1)}, u32[]{:S(2)}, u32[]{:S(2)}) %all-to-all-start) | async-done | bytes 1048608 | tf_op jit(solution)/shard_map/all_to_all | solution.py:305
  32.8 0.0 copy-start
  32.8 1.0 copy-done
  33.8 3.7 %gather.1 = f32[64,256]{1,0:T(8,128)} custom-call(bf16[64,64,128]{2,1,0:T(8,128)(2,1)} %bitcast.31, s32[1,256]{1,0:T(1,128)} %bitcast.38), custom_call_target="tpu_custom_call" | custom-call | tf_op jit(solution)/shard_map/gather/pallas_call | solution.py:52
  37.5 0.0 copy-start.1
  37.5 0.9 convert_element_type.23.refs_0_
  38.4 0.0 copy-start.2
  38.4 0.0 collective-permute-start
  38.5 0.0 copy-done.1
  38.5 1.2 %collective-permute-done.refs_1_ = bf16[64,256]{1,0:T(8,128)(2,1)S(1)} collective-permute-done((bf16[64,256]{1,0:T(8,128)(2,1)S(1)}, bf16[64,256]{1,0:T(8,128)(2,1)S(1)}, u32[]{:S(2)}, u32[]{:S(2)}) %collective-permute-start) | collective-permute-done | bytes 32800 | tf_op jit(solution)/shard_map/ppermute | solution.py:280
  39.6 0.0 copy-start.3
  39.7 0.6 copy-done.3
  40.3 1.2 %collective-permute-start.2 = (bf16[2,64,256]{2,1,0:T(8,128)(2,1)S(1)}, bf16[2,64,256]{2,1,0:T(8,128)(2,1)S(1)}, u32[]{:S(2)}, u32[]{:S(2)}) collective-permute-start(bf16[2,64,256]{2,1,0:T(8,128)(2,1)S(1)} %pad_maximum_fusion), channel_id=1, source_target_pairs={{0,1},{1,0},{2,3},{3,2},{4,5},{5,4},{6,7},{7,6},{8,9},{9,8},{10,11... | collective-permute-start | bytes 196616 | tf_op jit(solution)/shard_map/ppermute | solution.py:283
  41.5 0.0 collective-permute-done.5
  41.5 0.0 collective-permute-done.4
  41.5 0.0 copy-start.4
  41.5 0.3 collective-permute-start.6
  41.8 5.1 %collective-permute-start.3 = (bf16[64,256]{1,0:T(8,128)(2,1)S(1)}, bf16[64,256]{1,0:T(8,128)(2,1)S(1)}, u32[]{:S(2)}, u32[]{:S(2)}) collective-permute-start(bf16[64,256]{1,0:T(8,128)(2,1)S(1)} %convert_element_type.23.refs_0_), channel_id=1, source_target_pairs={{2,5},{3,4},{4,3},{5,2},{6,9},{7,8},{8,7},{9,6},{10,13},{11,12},{1... | collective-permute-start | bytes 98312 | tf_op jit(solution)/shard_map/ppermute | solution.py:291
  47.0 0.0 copy-done.2
  47.0 1.9 %collective-permute-start.1 = (bf16[64,256]{1,0:T(8,128)(2,1)S(1)}, bf16[64,256]{1,0:T(8,128)(2,1)S(1)}, u32[]{:S(2)}, u32[]{:S(2)}) collective-permute-start(bf16[64,256]{1,0:T(8,128)(2,1)S(1)} %convert_element_type.23.refs_0_), channel_id=1, source_target_pairs={{2,4},{4,2},{6,8},{8,6},{10,12},{12,10},{14,16},{16,14},{18,20},{2... | collective-permute-start | bytes 98312 | tf_op jit(solution)/shard_map/ppermute | solution.py:280
  48.9 0.0 collective-permute-done.2
  48.9 0.6 slice_bitcast_fusion
  49.5 0.0 copy-done.4
  49.5 0.0 collective-permute-done.6.refs_7_
  49.5 0.0 copy-start.7
  49.5 0.0 collective-permute-done.3.refs_5_
  49.6 0.0 copy-start.5
  49.6 2.6 %collective-permute-done.1.refs_2_ = bf16[64,256]{1,0:T(8,128)(2,1)S(1)} collective-permute-done((bf16[64,256]{1,0:T(8,128)(2,1)S(1)}, bf16[64,256]{1,0:T(8,128)(2,1)S(1)}, u32[]{:S(2)}, u32[]{:S(2)}) %collective-permute-start.1) | collective-permute-done | bytes 32800 | tf_op jit(solution)/shard_map/ppermute | solution.py:280
  52.2 0.0 copy-start.6
  52.2 0.0 copy-done.7
  52.2 0.0 copy-done.5
  52.2 0.6 copy-done.6
  52.8 13.8 %transform.1.mix_ref = bf16[2,64,512]{2,1,0:T(8,128)(2,1)} custom-call(s32[3]{0:T(128)} %pad_add_fusion.scal_ref, bf16[64,256]{1,0:T(8,128)(2,1)} %copy-done.2, bf16[64,256]{1,0:T(8,128)(2,1)} %copy-done.3, bf16[64,256]{1,0:T(8,128)(2,1)} %copy-done.6, bf16[64,256]{1,0:T(8,128)(2,1)} %get-tuple-element.8.refs_3_, bf16[64,256]{1,0:T(8,128)(2,1)} %get-tuple-element.7.refs_4_, ...), custom_call_target="tpu_custom_call" | custom-call | tf_op jit(solution)/shard_map/transform/pallas_call | solution.py:214
  66.6 5.5 %mix.1 = bf16[64,64,128]{2,1,0:T(8,128)(2,1)} custom-call(bf16[2,64,512]{2,1,0:T(8,128)(2,1)} %transform.1.mix_ref, bf16[64,64,128]{2,1,0:T(8,128)(2,1)} %bitcast.32), custom_call_target="tpu_custom_call" | custom-call | tf_op jit(solution)/shard_map/mix/pallas_call | solution.py:253
  72.1 31.8 %all_to_all.10 = bf16[16,4,2,32,128]{4,3,2,1,0:T(8,128)(2,1)S(1)} all-to-all(bf16[16,4,2,32,128]{4,3,2,1,0:T(8,128)(2,1)} %bitcast.33), channel_id=1, replica_groups=mesh['mem'=16,'gy'=2] {'mem'}, dimensions={0} | all-to-all | bytes 2097152 | tf_op jit(solution)/shard_map/all_to_all | solution.py:323
  104.0 1.1 %copy.8 = bf16[4,2,16,32,128]{4,3,2,1,0:T(8,128)(2,1)} copy(bf16[4,2,16,32,128]{4,3,1,0,2:T(8,128)(2,1)S(1)} %bitcast.34) | data formatting | bytes 2097152 | tf_op jit(solution)/shard_map/transpose | solution.py:324
  (8 shorter events, 0.1 us)
Async XLA Ops:
  2.3 30.5 %all-to-all-start = ((bf16[16,4,2,32,128]{4,3,2,1,0:T(8,128)(2,1)}), bf16[16,4,2,32,128]{4,3,2,1,0:T(8,128)(2,1)S(1)}, u32[]{:S(2)}, u32[]{:S(2)}) async-start(bf16[16,4,2,32,128]{4,3,2,1,0:T(8,128)(2,1)} %bitcast.28), calls=%async_computation | async-start | bytes 2097152 | tf_op jit(solution)/shard_map/all_to_all | solution.py:305
  10.3 0.7 copy-start.10
  11.0 0.7 copy-start.8
  11.7 0.7 copy-start.9
  12.4 29.1 %collective-permute-start.5 = (f32[8,256]{1,0:T(8,128)S(1)}, f32[8,256]{1,0:T(8,128)S(1)}, u32[]{:S(2)}, u32[]{:S(2)}) collective-permute-start(f32[8,256]{1,0:T(8,128)S(1)} %concatenate.3), channel_id=1, source_target_pairs={{2,4},{4,2},{6,8},{8,6},{10,12},{12,10},{14,16},{16,14},{18,20},{2... | collective-permute-start | bytes 24584 | tf_op jit(solution)/shard_map/ppermute | solution.py:280
  16.0 25.5 %collective-permute-start.4 = (f32[8,256]{1,0:T(8,128)S(1)}, f32[8,256]{1,0:T(8,128)S(1)}, u32[]{:S(2)}, u32[]{:S(2)}) collective-permute-start(f32[8,256]{1,0:T(8,128)S(1)} %concatenate.3), channel_id=1, source_target_pairs={{0,2},{2,0},{4,6},{6,4},{8,10},{10,8},{12,14},{14,12},{16,18},{18,... | collective-permute-start | bytes 24584 | tf_op jit(solution)/shard_map/ppermute | solution.py:280
  32.8 1.0 copy-start
  37.5 0.9 copy-start.1
  38.4 8.5 %copy-start.2 = (bf16[64,256]{1,0:T(8,128)(2,1)}, bf16[64,256]{1,0:T(8,128)(2,1)S(1)}, u32[]{:S(2)}) copy-start(bf16[64,256]{1,0:T(8,128)(2,1)S(1)} %convert_element_type.23.refs_0_) | copy-start | bytes 98308
  38.4 1.2 %collective-permute-start = (bf16[64,256]{1,0:T(8,128)(2,1)S(1)}, bf16[64,256]{1,0:T(8,128)(2,1)S(1)}, u32[]{:S(2)}, u32[]{:S(2)}) collective-permute-start(bf16[64,256]{1,0:T(8,128)(2,1)S(1)} %convert_element_type.23.refs_0_), channel_id=1, source_target_pairs={{0,2},{2,0},{4,6},{6,4},{8,10},{10,8},{12,14},{14,12},{16,18},{18,... | collective-permute-start | bytes 98312 | tf_op jit(solution)/shard_map/ppermute | solution.py:280
  39.6 0.6 copy-start.3
  40.3 8.7 %collective-permute-start.2 = (bf16[2,64,256]{2,1,0:T(8,128)(2,1)S(1)}, bf16[2,64,256]{2,1,0:T(8,128)(2,1)S(1)}, u32[]{:S(2)}, u32[]{:S(2)}) collective-permute-start(bf16[2,64,256]{2,1,0:T(8,128)(2,1)S(1)} %pad_maximum_fusion), channel_id=1, source_target_pairs={{0,1},{1,0},{2,3},{3,2},{4,5},{5,4},{6,7},{7,6},{8,9},{9,8},{10,11... | collective-permute-start | bytes 196616 | tf_op jit(solution)/shard_map/ppermute | solution.py:283
  41.5 8.0 %copy-start.4 = (f32[3,8,256]{2,1,0:T(8,128)}, f32[3,8,256]{2,1,0:T(8,128)S(1)}, u32[]{:S(2)}) copy-start(f32[3,8,256]{2,1,0:T(8,128)S(1)} %pad_maximum_fusion.1.refs_6_) | copy-start | bytes 73732
  41.5 8.0 %collective-permute-start.6 = (f32[3,8,256]{2,1,0:T(8,128)S(1)}, f32[3,8,256]{2,1,0:T(8,128)S(1)}, u32[]{:S(2)}, u32[]{:S(2)}) collective-permute-start(f32[3,8,256]{2,1,0:T(8,128)S(1)} %pad_maximum_fusion.1.refs_6_), channel_id=1, source_target_pairs={{0,1},{1,0},{2,3},{3,2},{4,5},{5,4},{6,7},{7,6},{8,9},{9,8},{10,11... | collective-permute-start | bytes 73736 | tf_op jit(solution)/shard_map/ppermute | solution.py:283
  41.8 7.7 %collective-permute-start.3 = (bf16[64,256]{1,0:T(8,128)(2,1)S(1)}, bf16[64,256]{1,0:T(8,128)(2,1)S(1)}, u32[]{:S(2)}, u32[]{:S(2)}) collective-permute-start(bf16[64,256]{1,0:T(8,128)(2,1)S(1)} %convert_element_type.23.refs_0_), channel_id=1, source_target_pairs={{2,5},{3,4},{4,3},{5,2},{6,9},{7,8},{8,7},{9,6},{10,13},{11,12},{1... | collective-permute-start | bytes 98312 | tf_op jit(solution)/shard_map/ppermute | solution.py:291
  47.0 5.2 %collective-permute-start.1 = (bf16[64,256]{1,0:T(8,128)(2,1)S(1)}, bf16[64,256]{1,0:T(8,128)(2,1)S(1)}, u32[]{:S(2)}, u32[]{:S(2)}) collective-permute-start(bf16[64,256]{1,0:T(8,128)(2,1)S(1)} %convert_element_type.23.refs_0_), channel_id=1, source_target_pairs={{2,4},{4,2},{6,8},{8,6},{10,12},{12,10},{14,16},{16,14},{18,20},{2... | collective-permute-start | bytes 98312 | tf_op jit(solution)/shard_map/ppermute | solution.py:280
  49.5 2.7 %copy-start.7 = (f32[3,8,256]{2,1,0:T(8,128)}, f32[3,8,256]{2,1,0:T(8,128)S(1)}, u32[]{:S(2)}) copy-start(f32[3,8,256]{2,1,0:T(8,128)S(1)} %collective-permute-done.6.refs_7_) | copy-start | bytes 73732
  49.6 2.7 %copy-start.5 = (bf16[64,256]{1,0:T(8,128)(2,1)}, bf16[64,256]{1,0:T(8,128)(2,1)S(1)}, u32[]{:S(2)}) copy-start(bf16[64,256]{1,0:T(8,128)(2,1)S(1)} %collective-permute-done.3.refs_5_) | copy-start | bytes 98308
  52.2 0.6 copy-start.6
where the time goes:
time: 106 us; the launch traced here: 105 us
  blocking collectives  31.8 us (30%)
  Pallas kernels  23 us (22%)
  starting transfers between devices  19.5 us (18%)
  waiting for transfers between devices  19.3 us (18%)
  local copies, waits for them, and re-layouts  8.25 us (8%)
  other arithmetic  1.62 us (2%)
  between operations  1.47 us (1%)
    all_to_all x1, blocking collectives, local(): lax.all_to_all(analysed, 'mem', split_axis=0, concat_axis=0, tiled=True)  31.8 us
    all_to_all x1, waiting for transfers between devices, local(): lax.all_to_all(chunks, 'mem', split_axis=0, concat_axis=0, tiled=True)  15.5 us
    pallas_call x1, Pallas kernels, transform_call(): pl.pallas_call(functools.partial(transform_kernel, num_y, (count_c, count...  13.8 us
    all_to_all x1, starting transfers between devices, local(): lax.all_to_all(chunks, 'mem', split_axis=0, concat_axis=0, tiled=True)  7.31 us
    pallas_call x1, Pallas kernels, mix_call(): pl.pallas_call(functools.partial(mix_kernel, count_c, count_r, cols), in_...  5.55 us
    ppermute x4, starting transfers between devices, swap_x(): return lax.ppermute(value, 'mem', swap_pairs(n_x, first))  5.53 us
    ppermute x1, starting transfers between devices, swap_xy(): return lax.ppermute(value, ('mem', 'gy'), pairs)  5.15 us
    unnamed x22, local copies, waits for them, and re-layouts  4.18 us
  transfers between devices with their start and end apart: 8, of which 3 were waited for; matrix products, arithmetic and copies ran while one was open for 2% of the time, Pallas kernels for 4%

commit v1 on v0

v1 whole, which is shorter than its diff:
```python
import functools
import math

import jax
import jax.numpy as jnp
from jax import lax
from jax.experimental import pallas as pl
from jax.experimental.pallas import tpu as pltpu
from jax.sharding import PartitionSpec as P


BLK = 16
NSI = 10
f32 = jnp.float32
bf16 = jnp.bfloat16
META = 8


VMEM = pltpu.MemorySpace.VMEM


def on_chip(*values):
    return [pltpu.with_memory_space_constraint(value, VMEM) for value in values]


def dot(a, b):
    return lax.dot_general(a, b, (((1,), (0,)), ((), ())), preferred_element_type=f32)


def dot_t(a, b):
    return lax.dot_general(a, b, (((1,), (1,)), ((), ())), preferred_element_type=f32)


def split3(x):
    high = x.astype(bf16)
    rest = x - high.astype(f32)
    mid = rest.astype(bf16)
    low = (rest - mid.astype(f32)).astype(bf16)
    return high, mid, low


def gather_kernel(x_ref, idx_ref, ens_ref):
    members, cells, rows = x_ref.shape
    slots = idx_ref.shape[1]
    idx = idx_ref[...]
    row = lax.rem(idx, rows)
    cell = lax.div(idx, rows)
    pick_row = jnp.where(lax.broadcasted_iota(jnp.int32, (rows, slots), 0) == row, 1.0, 0.0).astype(bf16)
    pick_cell = lax.broadcasted_iota(jnp.int32, (cells, slots), 0) == cell
    group = 16
    for first in range(0, members, group):
        found = dot(x_ref[first : first + group].reshape(group * cells, rows), pick_row)
        lines = [
            jnp.sum(jnp.where(pick_cell, found[k * cells : (k + 1) * cells], 0.0), axis=0, keepdims=True)
            for k in range(group)
        ]
        ens_ref[first : first + group, :] = jnp.concatenate(lines, axis=0).astype(bf16)


def gather_call(x, obs_slots):
    vmem = pl.BlockSpec(memory_space=pltpu.VMEM)
    return pl.pallas_call(
        gather_kernel,
        in_specs=[vmem, vmem],
        out_specs=vmem,
        out_shape=pltpu.VMEM((x.shape[0], obs_slots.shape[0]), bf16),
        name="gather",
    )(*on_chip(x), obs_slots[None])


def recursion_product(a, b, left):
    ah, am, al = a
    bh, bm, bl = b
    return dot(
        jnp.concatenate([ah, am, jnp.where(left, al, ah)], axis=1),
        jnp.concatenate([bh, bm, bh, bm, bh, bl], axis=0),
    )


def find_transforms(num_y, sizes, scal_ref, *refs):
    count_r, cols, rows = sizes
    ens_refs = refs[: 2 * num_y]
    meta_refs = refs[2 * num_y : 2 * num_y + 2]
    out_ref, lhs_ref, gram_ref, up_ref, low_ref = refs[2 * num_y + 2 :]
    members, slots = ens_refs[0].shape
    wide = 2 * members
    block_c = scal_ref[0].astype(f32)
    side = scal_ref[1].astype(f32)
    odd_y = scal_ref[2] == 1
    reach = scal_ref[3].astype(f32)
    reach_sq = reach * reach

    def prepare(ens_ref, meta):
        ens = ens_ref[...].astype(f32)
        centre = jnp.sum(ens, axis=0, keepdims=True) * (1.0 / members)
        spread = ens - centre
        sh, sm, sl = split3(spread)
        line = lax.broadcasted_iota(jnp.int32, (members, slots), 0)
        ih, im, il = (part.astype(f32) for part in split3(meta[0:1] - centre))
        extra = jnp.where(line == 0, ih, jnp.where(line == 1, im, jnp.where(line == 2, il, 0.0))).astype(bf16)
        return spread, jnp.concatenate([sh, sm, sl, extra], axis=0)

    def local_weight(meta, dx, dy, block_r):
        gap_c = dx * cols + meta[2:3] - (block_c * float(BLK) + (BLK - 1) / 2.0)
        gap_r = dy * rows + meta[3:4] - (block_r * float(BLK) + (BLK - 1) / 2.0)
        taper = jnp.maximum(1.0 - (gap_c * gap_c + gap_r * gap_r) / reach_sq, 0.0)
        return taper * taper * meta[1:2]

    def put(part, total, column, rho, spread):
        for level, piece in enumerate(split3(rho * spread)):
            start = level * total + part * members
            lhs_ref[start : start + members, column : column + slots] = piece

    def product(y, total, dy, block_r):
        sides = []
        for at, dx in enumerate((0.0, side)):
            meta = meta_refs[at][y]
            spread, rhs = prepare(ens_refs[2 * y + at], meta)
            rho = local_weight(meta, dx, dy, block_r)
            for r in range(total // members):
                put(r, total, at * slots, rho[r : r + 1], spread)
            sides.append(rhs)
        found = dot_t(lhs_ref[: 3 * total, :], jnp.concatenate(sides, axis=1))
        return found[:total] + found[total : 2 * total] + found[2 * total :]

    lines = lax.broadcasted_iota(jnp.int32, (count_r, slots), 0).astype(f32)
    gram_ref[...] = product(0, count_r * members, 0.0, lines).reshape(count_r, members, 4 * members)
    for y in range(1, num_y):
        above = jnp.logical_not(odd_y) if y == 1 else odd_y
        edge = jnp.where(above, count_r - 1, 0)
        gram_ref[edge] += product(y, members, jnp.where(above, 1.0, -1.0), edge.astype(f32))

    line = lax.broadcasted_iota(jnp.int32, (members, wide), 0)
    lane = lax.broadcasted_iota(jnp.int32, (members, wide), 1)
    left = lane < members
    half = jnp.where(lane == line, 1.0, 0.0)
    eye = jnp.where(lane == line + members, 1.0, half)
    blocks = range(count_r)

    def keep(ref, b, value):
        for part, piece in enumerate(split3(value)):
            ref[b, part] = piece

    def held(ref, b):
        return ref[b, 0], ref[b, 1], ref[b, 2]

    scales = []
    drives = []
    starts = []
    for b in blocks:
        found = gram_ref[b]
        high, tail = found[:, :wide], found[:, wide:]
        once = high + jnp.where(left, tail, 0.0)
        system = (members - 1.0) * eye + once + pltpu.roll(once, members, 1)
        drive = jnp.sum(jnp.where(left, 0.0, tail), axis=1, keepdims=True)
        drives.append(jnp.sum(drive * eye, axis=0, keepdims=True))
        scale = jnp.sum(jnp.sum(system * half, axis=1, keepdims=True), axis=0, keepdims=True)
        scales.append(scale)
        starts.append(system / scale)
    for b in blocks:
        factor = 1.5 * eye - 0.5 * starts[b]
        keep(low_ref, b, factor)
        keep(up_ref, b, recursion_product(split3(starts[b]), split3(factor), left))

    def sweep():
        factors = []
        for b in blocks:
            product = recursion_product(held(low_ref, b), held(up_ref, b), left)
            factors.append(split3(1.5 * eye - 0.5 * product))
        for b in blocks:
            upper = recursion_product(held(up_ref, b), factors[b], left)
            lower = recursion_product(factors[b], held(low_ref, b), left)
            keep(up_ref, b, upper)
            keep(low_ref, b, lower)

    together = 3

    def sweeps(_, carry):
        for _ in range(together):
            sweep()
        return carry

    lax.fori_loop(0, (NSI - 1) // together, sweeps, 0)

    mixed = []
    for b in blocks:
        lh, lm, ll = held(low_ref, b)
        lower = lh.astype(f32) + lm.astype(f32) + ll.astype(f32)
        inv_root = lower * lax.rsqrt(scales[b])
        first = jnp.sum(jnp.where(left, inv_root * drives[b], 0.0), axis=1, keepdims=True)
        shift = jnp.sum(inv_root * first, axis=0, keepdims=True)
        transform = math.sqrt(members - 1.0) * inv_root + shift
        mean = jnp.sum(jnp.where(left, transform, 0.0), axis=1, keepdims=True) * (1.0 / members)
        mixed.append(1.0 / members + transform - mean)
    for r in range(0, count_r, 2):
        out_ref[:, r * members : (r + 2) * members] = jnp.where(left, mixed[r], mixed[r + 1]).astype(bf16)


def turn_kernel(x_ref, out_ref):
    for start in range(0, x_ref.shape[1], BLK):
        part = x_ref[:, start : start + BLK, :].astype(f32)
        out_ref[start : start + BLK] = jnp.swapaxes(part, 0, 1).astype(bf16)


def turn_call(x):
    members, cells, rows = x.shape
    vmem = pl.BlockSpec(memory_space=pltpu.VMEM)
    return pl.pallas_call(
        turn_kernel,
        in_specs=[vmem],
        out_specs=vmem,
        out_shape=pltpu.VMEM((cells, members, rows), bf16),
        name="turn",
    )(*on_chip(x))


def mix_cells(levels, cols, scal_ref, mix_ref, x_ref, out_ref):
    _, members, rows = x_ref.shape
    lane_block = lax.broadcasted_iota(jnp.int32, (members, rows), 1) // BLK
    masks = [lane_block == r for r in range(rows // BLK)]
    zero = jnp.zeros((members, rows), bf16)
    mixing = mix_ref[...]
    for level in range(levels):
        start = level * cols + scal_ref[0] * BLK
        found = []
        for c in range(0, BLK, 2):
            wide = []
            for i in range(2):
                x = x_ref[start + c + i]
                wide.append(jnp.concatenate([jnp.where(m, x, zero) for m in masks], axis=0))
            both = dot(mixing, jnp.concatenate(wide, axis=1))
            found += [both[:, :rows], both[:, rows:]]
        out_ref[:, level * BLK : (level + 1) * BLK, :] = jnp.swapaxes(jnp.stack(found), 0, 1).astype(bf16)


def analyse_kernel(num_y, sizes, scal_ref, x_ref, *refs):
    levels, cols, rows = sizes
    column, beside, metas = refs[:num_y], refs[num_y : 2 * num_y], refs[2 * num_y : 2 * num_y + 2]
    out_ref, mix_ref = refs[2 * num_y + 2 : 2 * num_y + 4]
    ens = [ref for both in zip(column, beside) for ref in both]
    find_transforms(num_y, (rows // BLK, float(cols), float(rows)), scal_ref, *ens, *metas, *refs[2 * num_y + 3 :])
    mix_cells(levels, cols, scal_ref, mix_ref, x_ref, out_ref)


def analyse_call(scalars, tile, column, beside, metas, levels, cols):
    num_y = len(column)
    _, members, rows = tile.shape
    slots = column[0].shape[1]
    count_r = rows // BLK
    vmem = pl.BlockSpec(memory_space=pltpu.VMEM)
    return pl.pallas_call(
        functools.partial(analyse_kernel, num_y, (levels, cols, rows)),
        in_specs=[pl.BlockSpec(memory_space=pltpu.SMEM)] + [vmem] * (2 * num_y + 3),
        out_specs=vmem,
        out_shape=pltpu.VMEM((members, levels * BLK, rows), bf16),
        scratch_shapes=[
            pltpu.VMEM((members, count_r * members), bf16),
            pltpu.VMEM((3 * count_r * members, 2 * slots), bf16),
            pltpu.VMEM((count_r, members, 4 * members), f32),
            pltpu.VMEM((count_r, 3, members, 2 * members), bf16),
            pltpu.VMEM((count_r, 3, members, 2 * members), bf16),
        ],
        cost_estimate=pl.CostEstimate(flops=4 * 10**9, transcendentals=0, bytes_accessed=2 * 10**6),
        name="analyse",
    )(scalars, *on_chip(tile, *column, *beside, *metas))


def pack_kernel(state_ref, out_ref, sems):
    count, _, _, cols, _ = out_ref.shape
    copies = [
        pltpu.make_async_copy(state_ref.at[:, :, pl.ds(p * cols, cols), :], out_ref.at[p], sems.at[p]) for p in range(count)
    ]
    for copy in copies:
        copy.start()
    for copy in copies:
        copy.wait()


def pack_call(state, count, cols):
    held, levels, _, rows = state.shape
    return pl.pallas_call(
        pack_kernel,
        in_specs=[pl.BlockSpec(memory_space=pl.ANY)],
        out_specs=pl.BlockSpec(memory_space=pltpu.VMEM),
        out_shape=pltpu.VMEM((count, held, levels, cols, rows), bf16),
        scratch_shapes=[pltpu.SemaphoreType.DMA((count,))],
        name="pack",
    )(state)


def unpack_kernel(first_ref, second_ref, out_ref, sems):
    count, _, _, half, _ = first_ref.shape
    copies = []
    for p in range(count):
        for at, ref in enumerate((second_ref, first_ref) if p % 2 == 0 else (first_ref, second_ref)):
            start = (2 * p + at) * half
            copies.append(pltpu.make_async_copy(ref.at[p], out_ref.at[:, :, pl.ds(start, half), :], sems.at[2 * p + at]))
    for copy in copies:
        copy.start()
    for copy in copies:
        copy.wait()


def unpack_call(first, second):
    count, held, levels, half, rows = first.shape
    vmem = pl.BlockSpec(memory_space=pltpu.VMEM)
    return pl.pallas_call(
        unpack_kernel,
        in_specs=[vmem, vmem],
        out_specs=pl.BlockSpec(memory_space=pl.ANY),
        out_shape=jax.ShapeDtypeStruct((held, levels, 2 * count * half, rows), bf16),
        scratch_shapes=[pltpu.SemaphoreType.DMA((2 * count,))],
        name="unpack",
    )(*on_chip(first, second))


def swap_pairs(count, first):
    pairs = []
    for i in range(first, count - 1, 2):
        pairs += [(i, i + 1), (i + 1, i)]
    return pairs


def local(state, obs_index, obs_count, obs_value, obs_var, radius):
    n_x = lax.axis_size("mem")
    n_y = lax.axis_size("gy")
    held, levels, all_cols, rows = state.shape
    cols = all_cols // n_x
    members = held * n_x
    assert cols == 2 * BLK
    obs_slots = obs_index[0, 0]
    slots = obs_slots.shape[0]

    def swap_x(value, first):
        return lax.ppermute(value, "mem", swap_pairs(n_x, first))

    def swap_y(value, first):
        return lax.ppermute(value, "gy", swap_pairs(n_y, first))

    y_steps = [first for first in (0, 1) if swap_pairs(n_y, first)]

    live = jnp.arange(slots, dtype=jnp.int32) < obs_count[0, 0]
    weight = jnp.where(live, 1.0 / obs_var[0, 0], 0.0)
    col_pos = (obs_slots // rows % cols).astype(f32)
    row_pos = (obs_slots % rows).astype(f32)
    blank = jnp.zeros((META - 4, slots), f32)
    meta = jnp.concatenate([jnp.stack([obs_value[0, 0], weight, col_pos, row_pos]), blank], axis=0)
    meta_column = jnp.stack([meta] + [swap_y(meta, first) for first in y_steps])
    near_meta = swap_x(meta_column, 0)
    far_meta = swap_x(meta_column, 1)
    odd_x = lax.axis_index("mem") & 1
    odd_y = lax.axis_index("gy") & 1
    scalars = [
        jnp.stack([block_c, 2 * block_c - 1, odd_y, radius[0, 0]]).astype(jnp.int32) for block_c in (1 - odd_x, odd_x)
    ]

    tile = lax.all_to_all(pack_call(state, n_x, cols), "mem", split_axis=0, concat_axis=0, tiled=True)
    tile, meta_column, near_meta, scalars = lax.optimization_barrier((tile, meta_column, near_meta, scalars))
    tile = tile.reshape(members, levels * cols, rows)

    own = gather_call(tile, obs_slots)
    column = [own] + [swap_y(own, first) for first in y_steps]
    far_own = swap_x(own, 1)
    tile = turn_call(tile)
    near = [swap_x(ens, 0) for ens in column]

    def send_back(analysed):
        analysed = analysed.reshape(n_x, held, levels, BLK, rows)
        return lax.all_to_all(analysed, "mem", split_axis=0, concat_axis=0, tiled=True)

    analysed = analyse_call(scalars[0], tile, column, near, (meta_column, near_meta), levels, cols)
    first = send_back(analysed)
    far = [far_own] + [swap_y(far_own, step) for step in y_steps]
    analysed = analyse_call(scalars[1], tile, column, far, (meta_column, far_meta), levels, cols)
    second = send_back(analysed)
    return unpack_call(first, second)


def solution(mesh):
    in_specs = (
        P("mem", None, None, "gy"),
        P("mem", "gy", None),
        P("mem", "gy"),
        P("mem", "gy", None),
        P("mem", "gy", None),
        P("mem", "gy"),
    )
    out_specs = P("mem", None, None, "gy")
    return jax.shard_map(local, mesh=mesh, in_specs=in_specs, out_specs=out_specs, check_vma=False)
```

time: 106 us -> 104 us (0.981)
  starting transfers between devices: 19.5 us -> 27 us
  local copies, waits for them, and re-layouts: 8.25 us -> 2.03 us
  blocking collectives: 31.8 us -> 27.2 us
  waiting for transfers between devices: 19.3 us -> 23 us
  Pallas kernels: 23 us -> 21.5 us
    all_to_all x1 -> x2, starting transfers between devices: 7.31 us -> 14.3 us  [the longest x1 7.32 us: local(): lax.all_to_all(pack_call(state, n_x, cols), 'mem', split_axis=0, concat_a...]
    ppermute x1 -> x0, starting transfers between devices: 5.15 us -> none  [swap_xy(): return lax.ppermute(value, ('mem', 'gy'), pairs)]
    all_to_all x1, blocking collectives: 31.8 us -> 27.2 us  [send_back(): lax.all_to_all(analysed, 'mem', split_axis=0, concat_axis=0, tiled=True)]
    ppermute x4 -> x5, starting transfers between devices: 5.53 us -> 8.83 us  [swap_x(): return lax.ppermute(value, 'mem', swap_pairs(n_x, first))]
    ppermute x2 -> x3, waiting for transfers between devices: 0.01 us -> 2.73 us  [swap_y(): return lax.ppermute(value, 'gy', swap_pairs(n_y, first))]
    reshape x1 -> x0, local copies, waits for them, and re-layouts: 2.35 us -> none  [local(): state.reshape(held, levels, n_x, cols, rows).transpose(2, 0, 1, 3, 4)]
    ppermute x2 -> x3, starting transfers between devices: 1.53 us -> 3.84 us  [swap_y(): return lax.ppermute(value, 'gy', swap_pairs(n_y, first))]
    unnamed x22 -> x6, local copies, waits for them, and re-layouts: 4.18 us -> 2.01 us
  transfers between devices with their start and end apart: 8 -> 10, of which waited for: 3 -> 7; matrix products, arithmetic and copies ran while one was open for 2% -> 1% of each run, Pallas kernels for 4% -> 8%
where the time goes in v1:
time: 104 us; the launch traced here: 103 us
  blocking collectives  27.2 us (26%)
  starting transfers between devices  27 us (26%)
  waiting for transfers between devices  23 us (22%)
  Pallas kernels  21.5 us (21%)
  local copies, waits for them, and re-layouts  2.03 us (2%)
  between operations  1.41 us (1%)
    all_to_all x1, blocking collectives, send_back(): lax.all_to_all(analysed, 'mem', split_axis=0, concat_axis=0, tiled=True)  27.2 us
    pallas_call x2, Pallas kernels, analyse_call(): pl.pallas_call(functools.partial(analyse_kernel, num_y, (levels, cols, ro...  16 us
    all_to_all x1, waiting for transfers between devices, local(): lax.all_to_all(pack_call(state, n_x, cols), 'mem', split_axis=0, concat_a...  15.8 us
    ppermute x5, starting transfers between devices, swap_x(): return lax.ppermute(value, 'mem', swap_pairs(n_x, first))  8.83 us
    all_to_all x1, starting transfers between devices, local(): lax.all_to_all(pack_call(state, n_x, cols), 'mem', split_axis=0, concat_a...  7.32 us
    all_to_all x1, starting transfers between devices, send_back(): lax.all_to_all(analysed, 'mem', split_axis=0, concat_axis=0, tiled=True)  6.95 us
    ppermute x5, waiting for transfers between devices, swap_x(): return lax.ppermute(value, 'mem', swap_pairs(n_x, first))  4.52 us
    ppermute x3, starting transfers between devices, swap_y(): return lax.ppermute(value, 'gy', swap_pairs(n_y, first))  3.84 us
  transfers between devices with their start and end apart: 10, of which 7 were waited for; matrix products, arithmetic and copies ran while one was open for 1% of the time, Pallas kernels for 8%

profile of v1, /device:TPU:1, one launch (start us, length us, event | category | flops | bytes accessed | tf_op | source)
XLA Modules:
  0.0 102.8 jit_solution(7472158617521196583)
XLA Ops:
  0.0 2.3 %pack.1 = bf16[16,4,2,32,128]{4,3,2,1,0:T(8,128)(2,1)} custom-call(bf16[4,2,512,128]{3,2,1,0:T(8,128)(2,1)} %state_ref.1), custom_call_target="tpu_custom_call" | custom-call | tf_op jit(solution)/shard_map/pack/pallas_call | solution.py:281
  2.4 7.3 %all-to-all-start = ((bf16[16,4,2,32,128]{4,3,2,1,0:T(8,128)(2,1)}), bf16[16,4,2,32,128]{4,3,2,1,0:T(8,128)(2,1)S(1)}, u32[]{:S(2)}, u32[]{:S(2)}) async-start(bf16[16,4,2,32,128]{4,3,2,1,0:T(8,128)(2,1)} %pack.1), calls=%async_computation | async-start | bytes 2097152 | tf_op jit(solution)/shard_map/all_to_all | solution.py:357
  10.3 0.0 copy-start.2
  10.3 0.7 copy-done.2
  11.0 0.0 copy-start
  11.0 0.7 copy-done
  11.7 0.0 copy-start.1
  11.7 0.7 copy-done.1
  12.4 1.3 %collective-permute-start = (f32[8,256]{1,0:T(8,128)S(1)}, f32[8,256]{1,0:T(8,128)S(1)}, u32[]{:S(2)}, u32[]{:S(2)}) collective-permute-start(f32[8,256]{1,0:T(8,128)S(1)} %concatenate.3), channel_id=1, source_target_pairs={{0,1},{1,0},{2,3},{3,2},{4,5},{5,4},{6,7},{7,6},{8,9},{9,8},{10,11... | collective-permute-start | bytes 24584 | tf_op jit(solution)/shard_map/ppermute | solution.py:338
  14.4 0.9 collective-permute-done
  15.3 1.0 collective-permute-start.1
  16.2 0.7 add_add_fusion
  16.9 0.2 collective-permute-done.1.refs_5_
  17.1 15.8 %all-to-all-done = bf16[16,4,2,32,128]{4,3,2,1,0:T(8,128)(2,1)S(1)} async-done(((bf16[16,4,2,32,128]{4,3,2,1,0:T(8,128)(2,1)}), bf16[16,4,2,32,128]{4,3,2,1,0:T(8,128)(2,1)S(1)}, u32[]{:S(2)}, u32[]{:S(2)}) %all-to-all-start) | async-done | bytes 1048608 | tf_op jit(solution)/shard_map/all_to_all | solution.py:357
  32.9 1.4 %gather.1.refs_0_ = bf16[64,256]{1,0:T(8,128)(2,1)S(1)} custom-call(bf16[64,64,128]{2,1,0:T(8,128)(2,1)S(1)} %bitcast.21, s32[1,256]{1,0:T(1,128)} %bitcast.25), custom_call_target="tpu_custom_call" | custom-call | tf_op jit(solution)/shard_map/gather/pallas_call | solution.py:62
  34.3 1.3 %collective-permute-start.2 = (bf16[64,256]{1,0:T(8,128)(2,1)S(1)}, bf16[64,256]{1,0:T(8,128)(2,1)S(1)}, u32[]{:S(2)}, u32[]{:S(2)}) collective-permute-start(bf16[64,256]{1,0:T(8,128)(2,1)S(1)} %gather.1.refs_0_), channel_id=1, source_target_pairs={{0,1},{1,0},{2,3},{3,2},{4,5},{5,4},{6,7},{7,6},{8,9},{9,8},{10,11... | collective-permute-start | bytes 98312 | tf_op jit(solution)/shard_map/ppermute | solution.py:338
  35.6 0.1 collective-permute-start.3
  35.6 1.8 %collective-permute-done.2.refs_1_ = bf16[64,256]{1,0:T(8,128)(2,1)S(1)} collective-permute-done((bf16[64,256]{1,0:T(8,128)(2,1)S(1)}, bf16[64,256]{1,0:T(8,128)(2,1)S(1)}, u32[]{:S(2)}, u32[]{:S(2)}) %collective-permute-start.2) | collective-permute-done | bytes 32800 | tf_op jit(solution)/shard_map/ppermute | solution.py:338
  37.5 0.7 collective-permute-start.4
  38.1 0.5 turn.1.x_ref
  38.7 0.0 collective-permute-done.3.refs_2_
  38.7 0.3 collective-permute-done.4.refs_3_
  39.0 8.4 %analyse.2 = bf16[64,32,128]{2,1,0:T(8,128)(2,1)} custom-call(s32[4]{0:T(128)} %get-tuple-element.10.scal_ref, bf16[64,64,128]{2,1,0:T(8,128)(2,1)S(1)} %turn.1.x_ref, bf16[64,256]{1,0:T(8,128)(2,1)S(1)} %gather.1.refs_0_, bf16[64,256]{1,0:T(8,128)(2,1)S(1)} %collective-permute-done.2.refs_1_, bf16[64,256]{1,0:T(8,128)(2,1)S(1)} %collective-permute-done.3.refs_2_, ...), custom_call_target="tpu_custom_call" | custom-call | flops 4000000000 | bytes 2000000 | tf_op jit(solution)/shard_map/analyse/pallas_call | solution.py:251
  47.4 7.0 %all-to-all-start.1 = ((bf16[16,4,2,16,128]{4,3,2,1,0:T(8,128)(2,1)}), bf16[16,4,2,16,128]{4,3,2,1,0:T(8,128)(2,1)S(1)}, u32[]{:S(2)}, u32[]{:S(2)}) async-start(bf16[16,4,2,16,128]{4,3,2,1,0:T(8,128)(2,1)} %bitcast.13), calls=%async_computation.1 | async-start | bytes 1048576 | tf_op jit(solution)/shard_map/all_to_all | solution.py:369
  54.3 3.5 %collective-permute-start.5 = (bf16[64,256]{1,0:T(8,128)(2,1)S(1)}, bf16[64,256]{1,0:T(8,128)(2,1)S(1)}, u32[]{:S(2)}, u32[]{:S(2)}) collective-permute-start(bf16[64,256]{1,0:T(8,128)(2,1)S(1)} %gather.1.refs_0_), channel_id=1, source_target_pairs={{2,4},{4,2},{6,8},{8,6},{10,12},{12,10},{14,16},{16,14},{18,20},{2... | collective-permute-start | bytes 98312 | tf_op jit(solution)/shard_map/ppermute | solution.py:335
  57.9 2.2 %collective-permute-done.5.refs_2_ = bf16[64,256]{1,0:T(8,128)(2,1)S(1)} collective-permute-done((bf16[64,256]{1,0:T(8,128)(2,1)S(1)}, bf16[64,256]{1,0:T(8,128)(2,1)S(1)}, u32[]{:S(2)}, u32[]{:S(2)}) %collective-permute-start.5) | collective-permute-done | bytes 32800 | tf_op jit(solution)/shard_map/ppermute | solution.py:335
  60.1 1.2 %collective-permute-start.6 = (bf16[64,256]{1,0:T(8,128)(2,1)S(1)}, bf16[64,256]{1,0:T(8,128)(2,1)S(1)}, u32[]{:S(2)}, u32[]{:S(2)}) collective-permute-start(bf16[64,256]{1,0:T(8,128)(2,1)S(1)} %collective-permute-done.5.refs_2_), channel_id=1, source_target_pairs={{0,1},{1,0},{2,3},{3,2},{4,5},{5,4},{6,7},{7,6},{8,9},{9,8},{10,11... | collective-permute-start | bytes 98312 | tf_op jit(solution)/shard_map/ppermute | solution.py:338
  61.3 3.6 %collective-permute-start.7 = (f32[2,8,256]{2,1,0:T(8,128)S(1)}, f32[2,8,256]{2,1,0:T(8,128)S(1)}, u32[]{:S(2)}, u32[]{:S(2)}) collective-permute-start(f32[2,8,256]{2,1,0:T(8,128)S(1)} %pad_maximum_fusion.refs_4_), channel_id=1, source_target_pairs={{2,4},{4,2},{6,8},{8,6},{10,12},{12,10},{14,16},{16,14},{18,20},{2... | collective-permute-start | bytes 49160 | tf_op jit(solution)/shard_map/ppermute | solution.py:335
  65.0 1.8 %collective-permute-done.7.refs_5_ = f32[2,8,256]{2,1,0:T(8,128)S(1)} collective-permute-done((f32[2,8,256]{2,1,0:T(8,128)S(1)}, f32[2,8,256]{2,1,0:T(8,128)S(1)}, u32[]{:S(2)}, u32[]{:S(2)}) %collective-permute-start.7) | collective-permute-done | bytes 16416 | tf_op jit(solution)/shard_map/ppermute | solution.py:335
  66.7 0.0 collective-permute-done.6.refs_3_
  66.7 7.6 %analyse.3 = bf16[64,32,128]{2,1,0:T(8,128)(2,1)S(1)} custom-call(s32[4]{0:T(128)} %get-tuple-element.14.scal_ref, bf16[64,64,128]{2,1,0:T(8,128)(2,1)S(1)} %turn.1.x_ref, bf16[64,256]{1,0:T(8,128)(2,1)S(1)} %gather.1.refs_0_, bf16[64,256]{1,0:T(8,128)(2,1)S(1)} %collective-permute-done.2.refs_1_, bf16[64,256]{1,0:T(8,128)(2,1)S(1)} %collective-permute-done.5.refs_2_, ...), custom_call_target="tpu_custom_call" | custom-call | flops 4000000000 | bytes 2000000 | tf_op jit(solution)/shard_map/analyse/pallas_call | solution.py:251
  74.3 0.0 all-to-all-done.1.first_ref
  74.4 27.2 %all_to_all.15.second_ref = bf16[16,4,2,16,128]{4,3,2,1,0:T(8,128)(2,1)S(1)} all-to-all(bf16[16,4,2,16,128]{4,3,2,1,0:T(8,128)(2,1)S(1)} %bitcast.23), channel_id=1, replica_groups=mesh['mem'=16,'gy'=2] {'mem'}, dimensions={0} | all-to-all | bytes 1048576 | tf_op jit(solution)/shard_map/all_to_all | solution.py:369
  101.5 1.2 %unpack.1 = bf16[4,2,512,128]{3,2,1,0:T(8,128)(2,1)} custom-call(bf16[16,4,2,16,128]{4,3,2,1,0:T(8,128)(2,1)S(1)} %all-to-all-done.1.first_ref, bf16[16,4,2,16,128]{4,3,2,1,0:T(8,128)(2,1)S(1)} %all_to_all.15.second_ref), custom_call_target="tpu_custom_call" | custom-call | tf_op jit(solution)/shard_map/unpack/pallas_call | solution.py:307
  (6 shorter events, 0.1 us)
Async XLA Ops:
  2.4 30.5 %all-to-all-start = ((bf16[16,4,2,32,128]{4,3,2,1,0:T(8,128)(2,1)}), bf16[16,4,2,32,128]{4,3,2,1,0:T(8,128)(2,1)S(1)}, u32[]{:S(2)}, u32[]{:S(2)}) async-start(bf16[16,4,2,32,128]{4,3,2,1,0:T(8,128)(2,1)} %pack.1), calls=%async_computation | async-start | bytes 2097152 | tf_op jit(solution)/shard_map/all_to_all | solution.py:357
  10.3 0.7 copy-start.2
  11.0 0.7 copy-start
  11.7 0.7 copy-start.1
  12.4 2.9 %collective-permute-start = (f32[8,256]{1,0:T(8,128)S(1)}, f32[8,256]{1,0:T(8,128)S(1)}, u32[]{:S(2)}, u32[]{:S(2)}) collective-permute-start(f32[8,256]{1,0:T(8,128)S(1)} %concatenate.3), channel_id=1, source_target_pairs={{0,1},{1,0},{2,3},{3,2},{4,5},{5,4},{6,7},{7,6},{8,9},{9,8},{10,11... | collective-permute-start | bytes 24584 | tf_op jit(solution)/shard_map/ppermute | solution.py:338
  15.3 1.8 %collective-permute-start.1 = (f32[2,8,256]{2,1,0:T(8,128)S(1)}, f32[2,8,256]{2,1,0:T(8,128)S(1)}, u32[]{:S(2)}, u32[]{:S(2)}) collective-permute-start(f32[2,8,256]{2,1,0:T(8,128)S(1)} %pad_maximum_fusion.refs_4_), channel_id=1, source_target_pairs={{0,2},{2,0},{4,6},{6,4},{8,10},{10,8},{12,14},{14,12},{16,18},{18,... | collective-permute-start | bytes 49160 | tf_op jit(solution)/shard_map/ppermute | solution.py:335
  34.3 3.2 %collective-permute-start.2 = (bf16[64,256]{1,0:T(8,128)(2,1)S(1)}, bf16[64,256]{1,0:T(8,128)(2,1)S(1)}, u32[]{:S(2)}, u32[]{:S(2)}) collective-permute-start(bf16[64,256]{1,0:T(8,128)(2,1)S(1)} %gather.1.refs_0_), channel_id=1, source_target_pairs={{0,1},{1,0},{2,3},{3,2},{4,5},{5,4},{6,7},{7,6},{8,9},{9,8},{10,11... | collective-permute-start | bytes 98312 | tf_op jit(solution)/shard_map/ppermute | solution.py:338
  35.6 3.1 %collective-permute-start.3 = (bf16[64,256]{1,0:T(8,128)(2,1)S(1)}, bf16[64,256]{1,0:T(8,128)(2,1)S(1)}, u32[]{:S(2)}, u32[]{:S(2)}) collective-permute-start(bf16[64,256]{1,0:T(8,128)(2,1)S(1)} %gather.1.refs_0_), channel_id=1, source_target_pairs={{0,2},{2,0},{4,6},{6,4},{8,10},{10,8},{12,14},{14,12},{16,18},{18,... | collective-permute-start | bytes 98312 | tf_op jit(solution)/shard_map/ppermute | solution.py:335
  37.5 1.5 %collective-permute-start.4 = (bf16[64,256]{1,0:T(8,128)(2,1)S(1)}, bf16[64,256]{1,0:T(8,128)(2,1)S(1)}, u32[]{:S(2)}, u32[]{:S(2)}) collective-permute-start(bf16[64,256]{1,0:T(8,128)(2,1)S(1)} %collective-permute-done.2.refs_1_), channel_id=1, source_target_pairs={{0,2},{2,0},{4,6},{6,4},{8,10},{10,8},{12,14},{14,12},{16,18},{18,... | collective-permute-start | bytes 98312 | tf_op jit(solution)/shard_map/ppermute | solution.py:335
  47.4 27.0 %all-to-all-start.1 = ((bf16[16,4,2,16,128]{4,3,2,1,0:T(8,128)(2,1)}), bf16[16,4,2,16,128]{4,3,2,1,0:T(8,128)(2,1)S(1)}, u32[]{:S(2)}, u32[]{:S(2)}) async-start(bf16[16,4,2,16,128]{4,3,2,1,0:T(8,128)(2,1)} %bitcast.13), calls=%async_computation.1 | async-start | bytes 1048576 | tf_op jit(solution)/shard_map/all_to_all | solution.py:369
  54.3 5.8 %collective-permute-start.5 = (bf16[64,256]{1,0:T(8,128)(2,1)S(1)}, bf16[64,256]{1,0:T(8,128)(2,1)S(1)}, u32[]{:S(2)}, u32[]{:S(2)}) collective-permute-start(bf16[64,256]{1,0:T(8,128)(2,1)S(1)} %gather.1.refs_0_), channel_id=1, source_target_pairs={{2,4},{4,2},{6,8},{8,6},{10,12},{12,10},{14,16},{16,14},{18,20},{2... | collective-permute-start | bytes 98312 | tf_op jit(solution)/shard_map/ppermute | solution.py:335
  60.1 6.6 %collective-permute-start.6 = (bf16[64,256]{1,0:T(8,128)(2,1)S(1)}, bf16[64,256]{1,0:T(8,128)(2,1)S(1)}, u32[]{:S(2)}, u32[]{:S(2)}) collective-permute-start(bf16[64,256]{1,0:T(8,128)(2,1)S(1)} %collective-permute-done.5.refs_2_), channel_id=1, source_target_pairs={{0,1},{1,0},{2,3},{3,2},{4,5},{5,4},{6,7},{7,6},{8,9},{9,8},{10,11... | collective-permute-start | bytes 98312 | tf_op jit(solution)/shard_map/ppermute | solution.py:338
  61.3 5.4 %collective-permute-start.7 = (f32[2,8,256]{2,1,0:T(8,128)S(1)}, f32[2,8,256]{2,1,0:T(8,128)S(1)}, u32[]{:S(2)}, u32[]{:S(2)}) collective-permute-start(f32[2,8,256]{2,1,0:T(8,128)S(1)} %pad_maximum_fusion.refs_4_), channel_id=1, source_target_pairs={{2,4},{4,2},{6,8},{8,6},{10,12},{12,10},{14,16},{16,14},{18,20},{2... | collective-permute-start | bytes 49160 | tf_op jit(solution)/shard_map/ppermute | solution.py:335

commit v2 on v1

--- a/solution.py
+++ b/solution.py
@@ -77,6 +77,10 @@
     )
 
 
+def short_product(a, b):
+    return dot(jnp.concatenate([a[0], a[1]], axis=1), jnp.concatenate([b[0], b[1], b[0], b[1]], axis=0))
+
+
 def find_transforms(num_y, sizes, scal_ref, *refs):
     count_r, cols, rows = sizes
     ens_refs = refs[: 2 * num_y]
@@ -94,11 +98,8 @@
         ens = ens_ref[...].astype(f32)
         centre = jnp.sum(ens, axis=0, keepdims=True) * (1.0 / members)
         spread = ens - centre
-        sh, sm, sl = split3(spread)
-        line = lax.broadcasted_iota(jnp.int32, (members, slots), 0)
-        ih, im, il = (part.astype(f32) for part in split3(meta[0:1] - centre))
-        extra = jnp.where(line == 0, ih, jnp.where(line == 1, im, jnp.where(line == 2, il, 0.0))).astype(bf16)
-        return spread, jnp.concatenate([sh, sm, sl, extra], axis=0)
+        parts = [*split3(spread), jnp.zeros((members, slots), bf16)]
+        return spread, meta[0:1] - centre, jnp.concatenate(parts, axis=0)
 
     def local_weight(meta, dx, dy, block_r):
         gap_c = dx * cols + meta[2:3] - (block_c * float(BLK) + (BLK - 1) / 2.0)
@@ -111,24 +112,37 @@
             start = level * total + part * members
             lhs_ref[start : start + members, column : column + slots] = piece
 
-    def product(y, total, dy, block_r):
+    lines = lax.broadcasted_iota(jnp.int32, (count_r, slots), 0)
+
+    def product(y, total, dy, block_r, chosen):
         sides = []
+        forces = []
         for at, dx in enumerate((0.0, side)):
             meta = meta_refs[at][y]
-            spread, rhs = prepare(ens_refs[2 * y + at], meta)
+            spread, innovation, rhs = prepare(ens_refs[2 * y + at], meta)
             rho = local_weight(meta, dx, dy, block_r)
             for r in range(total // members):
                 put(r, total, at * slots, rho[r : r + 1], spread)
+            force = rho * innovation
+            forces.append(force if chosen is None else jnp.where(chosen, force, 0.0))
             sides.append(rhs)
-        found = dot_t(lhs_ref[: 3 * total, :], jnp.concatenate(sides, axis=1))
-        return found[:total] + found[total : 2 * total] + found[2 * total :]
-
-    lines = lax.broadcasted_iota(jnp.int32, (count_r, slots), 0).astype(f32)
-    gram_ref[...] = product(0, count_r * members, 0.0, lines).reshape(count_r, members, 4 * members)
+        rhs = jnp.concatenate(sides, axis=1)
+        force = [part.astype(f32) for part in split3(jnp.concatenate(forces, axis=1))]
+        drive = dot_t(jnp.concatenate(force, axis=0).astype(bf16), rhs)
+        drive = drive[:count_r] + drive[count_r : 2 * count_r] + drive[2 * count_r :]
+        found = dot_t(lhs_ref[: 3 * total, :], rhs)
+        return found[:total] + found[total : 2 * total] + found[2 * total :], drive
+
+    found, drive = product(0, count_r * members, 0.0, lines.astype(f32), None)
+    gram_ref[...] = found.reshape(count_r, members, 4 * members)
     for y in range(1, num_y):
         above = jnp.logical_not(odd_y) if y == 1 else odd_y
         edge = jnp.where(above, count_r - 1, 0)
-        gram_ref[edge] += product(y, members, jnp.where(above, 1.0, -1.0), edge.astype(f32))
+        found, more = product(y, members, jnp.where(above, 1.0, -1.0), edge.astype(f32), lines == edge)
+        gram_ref[edge] += found
+        drive += more
+    drive = drive[:, :wide] + drive[:, wide:]
+    drive = drive + pltpu.roll(drive, members, 1)
 
     line = lax.broadcasted_iota(jnp.int32, (members, wide), 0)
     lane = lax.broadcasted_iota(jnp.int32, (members, wide), 1)
@@ -149,12 +163,10 @@
     starts = []
     for b in blocks:
         found = gram_ref[b]
-        high, tail = found[:, :wide], found[:, wide:]
-        once = high + jnp.where(left, tail, 0.0)
+        once = found[:, :wide] + found[:, wide:]
         system = (members - 1.0) * eye + once + pltpu.roll(once, members, 1)
-        drive = jnp.sum(jnp.where(left, 0.0, tail), axis=1, keepdims=True)
-        drives.append(jnp.sum(drive * eye, axis=0, keepdims=True))
-        scale = jnp.sum(jnp.sum(system * half, axis=1, keepdims=True), axis=0, keepdims=True)
+        drives.append(drive[b : b + 1])
+        scale = jnp.sum(jnp.sum(system * half, axis=0, keepdims=True), axis=1, keepdims=True)
         scales.append(scale)
         starts.append(system / scale)
     for b in blocks:
@@ -162,31 +174,34 @@
         keep(low_ref, b, factor)
         keep(up_ref, b, recursion_product(split3(starts[b]), split3(factor), left))
 
-    def sweep():
-        factors = []
-        for b in blocks:
-            product = recursion_product(held(low_ref, b), held(up_ref, b), left)
-            factors.append(split3(1.5 * eye - 0.5 * product))
-        for b in blocks:
-            upper = recursion_product(held(up_ref, b), factors[b], left)
-            lower = recursion_product(factors[b], held(low_ref, b), left)
+    def first_stage(b):
+        return split3(1.5 * eye - 0.5 * short_product(held(low_ref, b), held(up_ref, b)))
+
+    def second_stage(b, factor, last):
+        lower = recursion_product(factor, held(low_ref, b), left)
+        if not last:
+            upper = recursion_product(held(up_ref, b), factor, left)
             keep(up_ref, b, upper)
             keep(low_ref, b, lower)
-
-    together = 3
-
-    def sweeps(_, carry):
-        for _ in range(together):
-            sweep()
-        return carry
-
-    lax.fori_loop(0, (NSI - 1) // together, sweeps, 0)
+        return lower
+
+    lag = count_r // 2
+    steps = (NSI - 1) * count_r
+    factors = {}
+    lowers = []
+    for step in range(steps + lag):
+        if step < steps:
+            factors[step] = first_stage(step % count_r)
+        done = step - lag
+        if done >= 0:
+            last = done >= steps - count_r
+            lower = second_stage(done % count_r, factors.pop(done), last)
+            if last:
+                lowers.append(lower)
 
     mixed = []
     for b in blocks:
-        lh, lm, ll = held(low_ref, b)
-        lower = lh.astype(f32) + lm.astype(f32) + ll.astype(f32)
-        inv_root = lower * lax.rsqrt(scales[b])
+        inv_root = lowers[b] * lax.rsqrt(scales[b])
         first = jnp.sum(jnp.where(left, inv_root * drives[b], 0.0), axis=1, keepdims=True)
         shift = jnp.sum(inv_root * first, axis=0, keepdims=True)
         transform = math.sqrt(members - 1.0) * inv_root + shift
@@ -217,8 +232,7 @@
 def mix_cells(levels, cols, scal_ref, mix_ref, x_ref, out_ref):
     _, members, rows = x_ref.shape
     lane_block = lax.broadcasted_iota(jnp.int32, (members, rows), 1) // BLK
-    masks = [lane_block == r for r in range(rows // BLK)]
-    zero = jnp.zeros((members, rows), bf16)
+    masks = [jnp.where(lane_block == r, 1.0, 0.0).astype(bf16) for r in range(rows // BLK)]
     mixing = mix_ref[...]
     for level in range(levels):
         start = level * cols + scal_ref[0] * BLK
@@ -227,7 +241,7 @@
             wide = []
             for i in range(2):
                 x = x_ref[start + c + i]
-                wide.append(jnp.concatenate([jnp.where(m, x, zero) for m in masks], axis=0))
+                wide.append(jnp.concatenate([x * mask for mask in masks], axis=0))
             both = dot(mixing, jnp.concatenate(wide, axis=1))
             found += [both[:, :rows], both[:, rows:]]
         out_ref[:, level * BLK : (level + 1) * BLK, :] = jnp.swapaxes(jnp.stack(found), 0, 1).astype(bf16)
@@ -265,53 +279,61 @@
     )(scalars, *on_chip(tile, *column, *beside, *metas))
 
 
-def pack_kernel(state_ref, out_ref, sems):
+def pack_kernel(state_ref, out_ref, held_ref, in_sems, out_sems):
     count, _, _, cols, _ = out_ref.shape
-    copies = [
-        pltpu.make_async_copy(state_ref.at[:, :, pl.ds(p * cols, cols), :], out_ref.at[p], sems.at[p]) for p in range(count)
+    loads = [
+        pltpu.make_async_copy(state_ref.at[:, :, pl.ds(p * cols, cols), :], held_ref.at[p], in_sems.at[p])
+        for p in range(count)
     ]
+    stores = [pltpu.make_async_copy(held_ref.at[p], out_ref.at[p], out_sems.at[p]) for p in range(count)]
+    for load in loads:
+        load.start()
+    for load, store in zip(loads, stores):
+        load.wait()
+        store.start()
+    for store in stores:
+        store.wait()
+
+
+def pack_call(state, count, cols):
+    held, levels, _, rows = state.shape
+    shape = (count, held, levels, cols, rows)
+    return pl.pallas_call(
+        pack_kernel,
+        in_specs=[pl.BlockSpec(memory_space=pl.ANY)],
+        out_specs=pl.BlockSpec(memory_space=pl.ANY),
+        out_shape=jax.ShapeDtypeStruct(shape, bf16),
+        scratch_shapes=[pltpu.VMEM(shape, bf16), pltpu.SemaphoreType.DMA((count,)), pltpu.SemaphoreType.DMA((count,))],
+        name="pack",
+    )(state)
+
+
+def unpack_kernel(near, half_ref, *refs):
+    out_ref, sems = refs[-2:]
+    count, _, _, half, _ = half_ref.shape
+    copies = []
+    for p in range(count):
+        start = (2 * p + (p + near) % 2) * half
+        copies.append(pltpu.make_async_copy(half_ref.at[p], out_ref.at[:, :, pl.ds(start, half), :], sems.at[p]))
     for copy in copies:
         copy.start()
     for copy in copies:
         copy.wait()
 
 
-def pack_call(state, count, cols):
-    held, levels, _, rows = state.shape
+def unpack_call(near, part, whole=None):
+    count, held, levels, half, rows = part.shape
+    anywhere = pl.BlockSpec(memory_space=pl.ANY)
+    others = [] if whole is None else [whole]
     return pl.pallas_call(
-        pack_kernel,
-        in_specs=[pl.BlockSpec(memory_space=pl.ANY)],
-        out_specs=pl.BlockSpec(memory_space=pltpu.VMEM),
-        out_shape=pltpu.VMEM((count, held, levels, cols, rows), bf16),
+        functools.partial(unpack_kernel, near),
+        in_specs=[pl.BlockSpec(memory_space=pltpu.VMEM)] + [anywhere] * len(others),
+        out_specs=anywhere,
+        out_shape=jax.ShapeDtypeStruct((held, levels, 2 * count * half, rows), bf16),
         scratch_shapes=[pltpu.SemaphoreType.DMA((count,))],
-        name="pack",
-    )(state)
-
-
-def unpack_kernel(first_ref, second_ref, out_ref, sems):
-    count, _, _, half, _ = first_ref.shape
-    copies = []
-    for p in range(count):
-        for at, ref in enumerate((second_ref, first_ref) if p % 2 == 0 else (first_ref, second_ref)):
-            start = (2 * p + at) * half
-            copies.append(pltpu.make_async_copy(ref.at[p], out_ref.at[:, :, pl.ds(start, half), :], sems.at[2 * p + at]))
-    for copy in copies:
-        copy.start()
-    for copy in copies:
-        copy.wait()
-
-
-def unpack_call(first, second):
-    count, held, levels, half, rows = first.shape
-    vmem = pl.BlockSpec(memory_space=pltpu.VMEM)
-    return pl.pallas_call(
-        unpack_kernel,
-        in_specs=[vmem, vmem],
-        out_specs=pl.BlockSpec(memory_space=pl.ANY),
-        out_shape=jax.ShapeDtypeStruct((held, levels, 2 * count * half, rows), bf16),
-        scratch_shapes=[pltpu.SemaphoreType.DMA((2 * count,))],
+        input_output_aliases={1: 0} if others else {},
         name="unpack",
-    )(*on_chip(first, second))
+    )(*on_chip(part), *others)
 
 
 def swap_pairs(count, first):
@@ -373,7 +395,8 @@
     far = [far_own] + [swap_y(far_own, step) for step in y_steps]
     analysed = analyse_call(scalars[1], tile, column, far, (meta_column, far_meta), levels, cols)
     second = send_back(analysed)
-    return unpack_call(first, second)
+    whole = unpack_call(1, first)
+    return unpack_call(0, second, whole)
 
 
 def solution(mesh):

time: 104 us -> 103 us (level)
  blocking collectives: 27.2 us -> 0 us
  starting transfers between devices: 27 us -> 40.5 us
  waiting for transfers between devices: 23 us -> 35.9 us
    all_to_all x1 -> x0, blocking collectives: 27.2 us -> none  [send_back(): lax.all_to_all(analysed, 'mem', split_axis=0, concat_axis=0, tiled=True)]
    all_to_all x1 -> x2, starting transfers between devices: 6.95 us -> 20.3 us  [send_back(): lax.all_to_all(analysed, 'mem', split_axis=0, concat_axis=0, tiled=True)]
    all_to_all x1 -> x2, waiting for transfers between devices: 0.01 us -> 13.1 us  [send_back(): lax.all_to_all(analysed, 'mem', split_axis=0, concat_axis=0, tiled=True)]
  transfers between devices with their start and end apart: 10 -> 11, of which waited for: 7 -> 8; matrix products, arithmetic and copies ran while one was open for 1% -> 1% of each run, Pallas kernels for 8% -> 9%
where the time goes in v2:
time: 103 us; the launch traced here: 102 us
  starting transfers between devices  40.5 us (39%)
  waiting for transfers between devices  35.9 us (35%)
  Pallas kernels  21.3 us (21%)
  local copies, waits for them, and re-layouts  2.03 us (2%)
  between operations  1.56 us (2%)
    all_to_all x2, starting transfers between devices, send_back(): lax.all_to_all(analysed, 'mem', split_axis=0, concat_axis=0, tiled=True)  20.3 us
    all_to_all x1, waiting for transfers between devices, local(): lax.all_to_all(pack_call(state, n_x, cols), 'mem', split_axis=0, concat_a...  15.8 us
    pallas_call x2, Pallas kernels, analyse_call(): pl.pallas_call(functools.partial(analyse_kernel, num_y, (levels, cols, ro...  15.4 us
    all_to_all x2, waiting for transfers between devices, send_back(): lax.all_to_all(analysed, 'mem', split_axis=0, concat_axis=0, tiled=True)  13.1 us
    ppermute x5, starting transfers between devices, swap_x(): return lax.ppermute(value, 'mem', swap_pairs(n_x, first))  9.02 us
    all_to_all x1, starting transfers between devices, local(): lax.all_to_all(pack_call(state, n_x, cols), 'mem', split_axis=0, concat_a...  7.32 us
    ppermute x5, waiting for transfers between devices, swap_x(): return lax.ppermute(value, 'mem', swap_pairs(n_x, first))  4.33 us
    ppermute x3, starting transfers between devices, swap_y(): return lax.ppermute(value, 'gy', swap_pairs(n_y, first))  3.84 us
  transfers between devices with their start and end apart: 11, of which 8 were waited for; matrix products, arithmetic and copies ran while one was open for 1% of the time, Pallas kernels for 9%

profile of v2, /device:TPU:1, one launch (start us, length us, event | category | flops | bytes accessed | tf_op | source)
XLA Modules:
  0.0 102.1 jit_solution(116401937313540092)
XLA Ops:
  0.0 2.2 %pack.1 = bf16[16,4,2,32,128]{4,3,2,1,0:T(8,128)(2,1)} custom-call(bf16[4,2,512,128]{3,2,1,0:T(8,128)(2,1)} %state_ref.1), custom_call_target="tpu_custom_call" | custom-call | tf_op jit(solution)/shard_map/pack/pallas_call | solution.py:301
  2.2 7.3 %all-to-all-start = ((bf16[16,4,2,32,128]{4,3,2,1,0:T(8,128)(2,1)}), bf16[16,4,2,32,128]{4,3,2,1,0:T(8,128)(2,1)S(1)}, u32[]{:S(2)}, u32[]{:S(2)}) async-start(bf16[16,4,2,32,128]{4,3,2,1,0:T(8,128)(2,1)} %pack.1), calls=%async_computation | async-start | bytes 2097152 | tf_op jit(solution)/shard_map/all_to_all | solution.py:379
  10.1 0.0 copy-start.2
  10.1 0.7 copy-done.2
  10.8 0.0 copy-start
  10.8 0.7 copy-done
  11.5 0.0 copy-start.1
  11.6 0.7 copy-done.1
  12.2 1.3 %collective-permute-start = (f32[8,256]{1,0:T(8,128)S(1)}, f32[8,256]{1,0:T(8,128)S(1)}, u32[]{:S(2)}, u32[]{:S(2)}) collective-permute-start(f32[8,256]{1,0:T(8,128)S(1)} %concatenate.3), channel_id=1, source_target_pairs={{0,1},{1,0},{2,3},{3,2},{4,5},{5,4},{6,7},{7,6},{8,9},{9,8},{10,11... | collective-permute-start | bytes 24584 | tf_op jit(solution)/shard_map/ppermute | solution.py:360
  14.2 0.9 collective-permute-done
  15.1 1.0 collective-permute-start.1
  16.1 0.7 add_add_fusion
  16.7 0.2 collective-permute-done.1.refs_5_
  16.9 15.8 %all-to-all-done = bf16[16,4,2,32,128]{4,3,2,1,0:T(8,128)(2,1)S(1)} async-done(((bf16[16,4,2,32,128]{4,3,2,1,0:T(8,128)(2,1)}), bf16[16,4,2,32,128]{4,3,2,1,0:T(8,128)(2,1)S(1)}, u32[]{:S(2)}, u32[]{:S(2)}) %all-to-all-start) | async-done | bytes 1048608 | tf_op jit(solution)/shard_map/all_to_all | solution.py:379
  32.7 1.4 %gather.1.refs_0_ = bf16[64,256]{1,0:T(8,128)(2,1)S(1)} custom-call(bf16[64,64,128]{2,1,0:T(8,128)(2,1)S(1)} %bitcast.21, s32[1,256]{1,0:T(1,128)} %bitcast.24), custom_call_target="tpu_custom_call" | custom-call | tf_op jit(solution)/shard_map/gather/pallas_call | solution.py:62
  34.1 1.3 %collective-permute-start.2 = (bf16[64,256]{1,0:T(8,128)(2,1)S(1)}, bf16[64,256]{1,0:T(8,128)(2,1)S(1)}, u32[]{:S(2)}, u32[]{:S(2)}) collective-permute-start(bf16[64,256]{1,0:T(8,128)(2,1)S(1)} %gather.1.refs_0_), channel_id=1, source_target_pairs={{0,1},{1,0},{2,3},{3,2},{4,5},{5,4},{6,7},{7,6},{8,9},{9,8},{10,11... | collective-permute-start | bytes 98312 | tf_op jit(solution)/shard_map/ppermute | solution.py:360
  35.4 0.1 collective-permute-start.6
  35.4 1.8 %collective-permute-done.2.refs_1_ = bf16[64,256]{1,0:T(8,128)(2,1)S(1)} collective-permute-done((bf16[64,256]{1,0:T(8,128)(2,1)S(1)}, bf16[64,256]{1,0:T(8,128)(2,1)S(1)}, u32[]{:S(2)}, u32[]{:S(2)}) %collective-permute-start.2) | collective-permute-done | bytes 32800 | tf_op jit(solution)/shard_map/ppermute | solution.py:360
  37.3 0.7 collective-permute-start.7
  37.9 0.5 turn.1.x_ref
  38.5 0.0 collective-permute-done.6.refs_2_
  38.5 0.3 collective-permute-done.7.refs_3_
  38.8 7.7 %analyse.3 = bf16[64,32,128]{2,1,0:T(8,128)(2,1)} custom-call(s32[4]{0:T(128)} %get-tuple-element.13.scal_ref, bf16[64,64,128]{2,1,0:T(8,128)(2,1)S(1)} %turn.1.x_ref, bf16[64,256]{1,0:T(8,128)(2,1)S(1)} %gather.1.refs_0_, bf16[64,256]{1,0:T(8,128)(2,1)S(1)} %collective-permute-done.2.refs_1_, bf16[64,256]{1,0:T(8,128)(2,1)S(1)} %collective-permute-done.6.refs_2_, ...), custom_call_target="tpu_custom_call" | custom-call | flops 4000000000 | bytes 2000000 | tf_op jit(solution)/shard_map/analyse/pallas_call | solution.py:265
  46.5 7.0 %all-to-all-start.2 = ((bf16[16,4,2,16,128]{4,3,2,1,0:T(8,128)(2,1)}), bf16[16,4,2,16,128]{4,3,2,1,0:T(8,128)(2,1)S(1)}, u32[]{:S(2)}, u32[]{:S(2)}) async-start(bf16[16,4,2,16,128]{4,3,2,1,0:T(8,128)(2,1)} %bitcast.14), calls=%async_computation.2 | async-start | bytes 1048576 | tf_op jit(solution)/shard_map/all_to_all | solution.py:391
  53.5 3.5 %collective-permute-start.3 = (bf16[64,256]{1,0:T(8,128)(2,1)S(1)}, bf16[64,256]{1,0:T(8,128)(2,1)S(1)}, u32[]{:S(2)}, u32[]{:S(2)}) collective-permute-start(bf16[64,256]{1,0:T(8,128)(2,1)S(1)} %gather.1.refs_0_), channel_id=1, source_target_pairs={{2,4},{4,2},{6,8},{8,6},{10,12},{12,10},{14,16},{16,14},{18,20},{2... | collective-permute-start | bytes 98312 | tf_op jit(solution)/shard_map/ppermute | solution.py:357
  57.0 2.2 %collective-permute-done.3.refs_2_ = bf16[64,256]{1,0:T(8,128)(2,1)S(1)} collective-permute-done((bf16[64,256]{1,0:T(8,128)(2,1)S(1)}, bf16[64,256]{1,0:T(8,128)(2,1)S(1)}, u32[]{:S(2)}, u32[]{:S(2)}) %collective-permute-start.3) | collective-permute-done | bytes 32800 | tf_op jit(solution)/shard_map/ppermute | solution.py:357
  59.2 1.2 %collective-permute-start.4 = (bf16[64,256]{1,0:T(8,128)(2,1)S(1)}, bf16[64,256]{1,0:T(8,128)(2,1)S(1)}, u32[]{:S(2)}, u32[]{:S(2)}) collective-permute-start(bf16[64,256]{1,0:T(8,128)(2,1)S(1)} %collective-permute-done.3.refs_2_), channel_id=1, source_target_pairs={{0,1},{1,0},{2,3},{3,2},{4,5},{5,4},{6,7},{7,6},{8,9},{9,8},{10,11... | collective-permute-start | bytes 98312 | tf_op jit(solution)/shard_map/ppermute | solution.py:360
  60.5 3.8 %collective-permute-start.5 = (f32[2,8,256]{2,1,0:T(8,128)S(1)}, f32[2,8,256]{2,1,0:T(8,128)S(1)}, u32[]{:S(2)}, u32[]{:S(2)}) collective-permute-start(f32[2,8,256]{2,1,0:T(8,128)S(1)} %pad_maximum_fusion.refs_4_), channel_id=1, source_target_pairs={{2,4},{4,2},{6,8},{8,6},{10,12},{12,10},{14,16},{16,14},{18,20},{2... | collective-permute-start | bytes 49160 | tf_op jit(solution)/shard_map/ppermute | solution.py:357
  64.3 1.6 %collective-permute-done.5.refs_5_ = f32[2,8,256]{2,1,0:T(8,128)S(1)} collective-permute-done((f32[2,8,256]{2,1,0:T(8,128)S(1)}, f32[2,8,256]{2,1,0:T(8,128)S(1)}, u32[]{:S(2)}, u32[]{:S(2)}) %collective-permute-start.5) | collective-permute-done | bytes 16416 | tf_op jit(solution)/shard_map/ppermute | solution.py:357
  65.9 0.0 collective-permute-done.4.refs_3_
  65.9 7.7 %analyse.2 = bf16[64,32,128]{2,1,0:T(8,128)(2,1)} custom-call(s32[4]{0:T(128)} %get-tuple-element.10.scal_ref, bf16[64,64,128]{2,1,0:T(8,128)(2,1)S(1)} %turn.1.x_ref, bf16[64,256]{1,0:T(8,128)(2,1)S(1)} %gather.1.refs_0_, bf16[64,256]{1,0:T(8,128)(2,1)S(1)} %collective-permute-done.2.refs_1_, bf16[64,256]{1,0:T(8,128)(2,1)S(1)} %collective-permute-done.3.refs_2_, ...), custom_call_target="tpu_custom_call" | custom-call | flops 4000000000 | bytes 2000000 | tf_op jit(solution)/shard_map/analyse/pallas_call | solution.py:265
  73.6 0.0 all-to-all-done.2.half_ref
  73.6 13.4 %all-to-all-start.1 = ((bf16[16,4,2,16,128]{4,3,2,1,0:T(8,128)(2,1)}), bf16[16,4,2,16,128]{4,3,2,1,0:T(8,128)(2,1)S(1)}, u32[]{:S(2)}, u32[]{:S(2)}) async-start(bf16[16,4,2,16,128]{4,3,2,1,0:T(8,128)(2,1)} %bitcast.13), calls=%async_computation.1 | async-start | bytes 1048576 | tf_op jit(solution)/shard_map/all_to_all | solution.py:391
  87.0 0.9 unpack.2.refs_0_
  87.9 13.1 %all-to-all-done.1.half_ref = bf16[16,4,2,16,128]{4,3,2,1,0:T(8,128)(2,1)S(1)} async-done(((bf16[16,4,2,16,128]{4,3,2,1,0:T(8,128)(2,1)}), bf16[16,4,2,16,128]{4,3,2,1,0:T(8,128)(2,1)S(1)}, u32[]{:S(2)}, u32[]{:S(2)}) %all-to-all-start.1) | async-done | bytes 524320 | tf_op jit(solution)/shard_map/all_to_all | solution.py:391
  101.0 0.9 unpack.3
  (6 shorter events, 0.1 us)
Async XLA Ops:
  2.2 30.5 %all-to-all-start = ((bf16[16,4,2,32,128]{4,3,2,1,0:T(8,128)(2,1)}), bf16[16,4,2,32,128]{4,3,2,1,0:T(8,128)(2,1)S(1)}, u32[]{:S(2)}, u32[]{:S(2)}) async-start(bf16[16,4,2,32,128]{4,3,2,1,0:T(8,128)(2,1)} %pack.1), calls=%async_computation | async-start | bytes 2097152 | tf_op jit(solution)/shard_map/all_to_all | solution.py:379
  10.1 0.7 copy-start.2
  10.8 0.7 copy-start
  11.5 0.7 copy-start.1
  12.2 2.9 %collective-permute-start = (f32[8,256]{1,0:T(8,128)S(1)}, f32[8,256]{1,0:T(8,128)S(1)}, u32[]{:S(2)}, u32[]{:S(2)}) collective-permute-start(f32[8,256]{1,0:T(8,128)S(1)} %concatenate.3), channel_id=1, source_target_pairs={{0,1},{1,0},{2,3},{3,2},{4,5},{5,4},{6,7},{7,6},{8,9},{9,8},{10,11... | collective-permute-start | bytes 24584 | tf_op jit(solution)/shard_map/ppermute | solution.py:360
  15.1 1.8 %collective-permute-start.1 = (f32[2,8,256]{2,1,0:T(8,128)S(1)}, f32[2,8,256]{2,1,0:T(8,128)S(1)}, u32[]{:S(2)}, u32[]{:S(2)}) collective-permute-start(f32[2,8,256]{2,1,0:T(8,128)S(1)} %pad_maximum_fusion.refs_4_), channel_id=1, source_target_pairs={{0,2},{2,0},{4,6},{6,4},{8,10},{10,8},{12,14},{14,12},{16,18},{18,... | collective-permute-start | bytes 49160 | tf_op jit(solution)/shard_map/ppermute | solution.py:357
  34.1 3.2 %collective-permute-start.2 = (bf16[64,256]{1,0:T(8,128)(2,1)S(1)}, bf16[64,256]{1,0:T(8,128)(2,1)S(1)}, u32[]{:S(2)}, u32[]{:S(2)}) collective-permute-start(bf16[64,256]{1,0:T(8,128)(2,1)S(1)} %gather.1.refs_0_), channel_id=1, source_target_pairs={{0,1},{1,0},{2,3},{3,2},{4,5},{5,4},{6,7},{7,6},{8,9},{9,8},{10,11... | collective-permute-start | bytes 98312 | tf_op jit(solution)/shard_map/ppermute | solution.py:360
  35.4 3.1 %collective-permute-start.6 = (bf16[64,256]{1,0:T(8,128)(2,1)S(1)}, bf16[64,256]{1,0:T(8,128)(2,1)S(1)}, u32[]{:S(2)}, u32[]{:S(2)}) collective-permute-start(bf16[64,256]{1,0:T(8,128)(2,1)S(1)} %gather.1.refs_0_), channel_id=1, source_target_pairs={{0,2},{2,0},{4,6},{6,4},{8,10},{10,8},{12,14},{14,12},{16,18},{18,... | collective-permute-start | bytes 98312 | tf_op jit(solution)/shard_map/ppermute | solution.py:357
  37.3 1.5 %collective-permute-start.7 = (bf16[64,256]{1,0:T(8,128)(2,1)S(1)}, bf16[64,256]{1,0:T(8,128)(2,1)S(1)}, u32[]{:S(2)}, u32[]{:S(2)}) collective-permute-start(bf16[64,256]{1,0:T(8,128)(2,1)S(1)} %collective-permute-done.2.refs_1_), channel_id=1, source_target_pairs={{0,2},{2,0},{4,6},{6,4},{8,10},{10,8},{12,14},{14,12},{16,18},{18,... | collective-permute-start | bytes 98312 | tf_op jit(solution)/shard_map/ppermute | solution.py:357
  46.5 27.1 %all-to-all-start.2 = ((bf16[16,4,2,16,128]{4,3,2,1,0:T(8,128)(2,1)}), bf16[16,4,2,16,128]{4,3,2,1,0:T(8,128)(2,1)S(1)}, u32[]{:S(2)}, u32[]{:S(2)}) async-start(bf16[16,4,2,16,128]{4,3,2,1,0:T(8,128)(2,1)} %bitcast.14), calls=%async_computation.2 | async-start | bytes 1048576 | tf_op jit(solution)/shard_map/all_to_all | solution.py:391
  53.5 5.8 %collective-permute-start.3 = (bf16[64,256]{1,0:T(8,128)(2,1)S(1)}, bf16[64,256]{1,0:T(8,128)(2,1)S(1)}, u32[]{:S(2)}, u32[]{:S(2)}) collective-permute-start(bf16[64,256]{1,0:T(8,128)(2,1)S(1)} %gather.1.refs_0_), channel_id=1, source_target_pairs={{2,4},{4,2},{6,8},{8,6},{10,12},{12,10},{14,16},{16,14},{18,20},{2... | collective-permute-start | bytes 98312 | tf_op jit(solution)/shard_map/ppermute | solution.py:357
  59.2 6.6 %collective-permute-start.4 = (bf16[64,256]{1,0:T(8,128)(2,1)S(1)}, bf16[64,256]{1,0:T(8,128)(2,1)S(1)}, u32[]{:S(2)}, u32[]{:S(2)}) collective-permute-start(bf16[64,256]{1,0:T(8,128)(2,1)S(1)} %collective-permute-done.3.refs_2_), channel_id=1, source_target_pairs={{0,1},{1,0},{2,3},{3,2},{4,5},{5,4},{6,7},{7,6},{8,9},{9,8},{10,11... | collective-permute-start | bytes 98312 | tf_op jit(solution)/shard_map/ppermute | solution.py:360
  60.5 5.4 %collective-permute-start.5 = (f32[2,8,256]{2,1,0:T(8,128)S(1)}, f32[2,8,256]{2,1,0:T(8,128)S(1)}, u32[]{:S(2)}, u32[]{:S(2)}) collective-permute-start(f32[2,8,256]{2,1,0:T(8,128)S(1)} %pad_maximum_fusion.refs_4_), channel_id=1, source_target_pairs={{2,4},{4,2},{6,8},{8,6},{10,12},{12,10},{14,16},{16,14},{18,20},{2... | collective-permute-start | bytes 49160 | tf_op jit(solution)/shard_map/ppermute | solution.py:357
  73.6 27.4 %all-to-all-start.1 = ((bf16[16,4,2,16,128]{4,3,2,1,0:T(8,128)(2,1)}), bf16[16,4,2,16,128]{4,3,2,1,0:T(8,128)(2,1)S(1)}, u32[]{:S(2)}, u32[]{:S(2)}) async-start(bf16[16,4,2,16,128]{4,3,2,1,0:T(8,128)(2,1)} %bitcast.13), calls=%async_computation.1 | async-start | bytes 1048576 | tf_op jit(solution)/shard_map/all_to_all | solution.py:391

commit v3 on v2

--- a/solution.py
+++ b/solution.py
@@ -13,6 +13,7 @@
 NSI = 10
 f32 = jnp.float32
 bf16 = jnp.bfloat16
+PITCH = BLK + 8
 META = 8
 
 
@@ -65,7 +66,7 @@
         out_specs=vmem,
         out_shape=pltpu.VMEM((x.shape[0], obs_slots.shape[0]), bf16),
         name="gather",
-    )(*on_chip(x), obs_slots[None])
+    )(*on_chip(x, obs_slots[None]))
 
 
 def recursion_product(a, b, left):
@@ -81,17 +82,17 @@
     return dot(jnp.concatenate([a[0], a[1]], axis=1), jnp.concatenate([b[0], b[1], b[0], b[1]], axis=0))
 
 
-def find_transforms(num_y, sizes, scal_ref, *refs):
+def find_transforms(num_y, sizes, block_c, *refs):
     count_r, cols, rows = sizes
     ens_refs = refs[: 2 * num_y]
     meta_refs = refs[2 * num_y : 2 * num_y + 2]
     out_ref, lhs_ref, gram_ref, up_ref, low_ref = refs[2 * num_y + 2 :]
     members, slots = ens_refs[0].shape
     wide = 2 * members
-    block_c = scal_ref[0].astype(f32)
-    side = scal_ref[1].astype(f32)
-    odd_y = scal_ref[2] == 1
-    reach = scal_ref[3].astype(f32)
+    side = (2 * block_c - 1).astype(f32)
+    block_c = block_c.astype(f32)
+    odd_y = lax.rem(lax.axis_index("gy"), 2) == 1
+    reach = meta_refs[0][0, 4:5]
     reach_sq = reach * reach
 
     def prepare(ens_ref, meta):
@@ -229,54 +230,65 @@
     )(*on_chip(x))
 
 
-def mix_cells(levels, cols, scal_ref, mix_ref, x_ref, out_ref):
+def mix_cells(levels, cols, block_c, mix_ref, x_ref, out_ref, held_ref, ready_ref, sems):
     _, members, rows = x_ref.shape
     lane_block = lax.broadcasted_iota(jnp.int32, (members, rows), 1) // BLK
     masks = [jnp.where(lane_block == r, 1.0, 0.0).astype(bf16) for r in range(rows // BLK)]
     mixing = mix_ref[...]
+    copies = []
     for level in range(levels):
-        start = level * cols + scal_ref[0] * BLK
-        found = []
+        start = level * cols + block_c * BLK
         for c in range(0, BLK, 2):
             wide = []
             for i in range(2):
                 x = x_ref[start + c + i]
                 wide.append(jnp.concatenate([x * mask for mask in masks], axis=0))
             both = dot(mixing, jnp.concatenate(wide, axis=1))
-            found += [both[:, :rows], both[:, rows:]]
-        out_ref[:, level * BLK : (level + 1) * BLK, :] = jnp.swapaxes(jnp.stack(found), 0, 1).astype(bf16)
-
-
-def analyse_kernel(num_y, sizes, scal_ref, x_ref, *refs):
+            for i in range(2):
+                held_ref[level, pl.ds(c + i, members, stride=PITCH), :] = both[:, i * rows : (i + 1) * rows]
+        mixed = held_ref[level].reshape(members, PITCH, rows)[:, :BLK, :]
+        ready_ref[level] = mixed.astype(bf16)
+        part = out_ref.at[:, pl.ds(level * BLK, BLK), :]
+        copies.append(pltpu.make_async_copy(ready_ref.at[level], part, sems.at[level]))
+        copies[-1].start()
+    for copy in copies:
+        copy.wait()
+
+
+def analyse_kernel(num_y, far, sizes, x_ref, *refs):
     levels, cols, rows = sizes
+    block_c = lax.rem(lax.axis_index("mem") + (0 if far else 1), 2)
     column, beside, metas = refs[:num_y], refs[num_y : 2 * num_y], refs[2 * num_y : 2 * num_y + 2]
     out_ref, mix_ref = refs[2 * num_y + 2 : 2 * num_y + 4]
     ens = [ref for both in zip(column, beside) for ref in both]
-    find_transforms(num_y, (rows // BLK, float(cols), float(rows)), scal_ref, *ens, *metas, *refs[2 * num_y + 3 :])
-    mix_cells(levels, cols, scal_ref, mix_ref, x_ref, out_ref)
-
-
-def analyse_call(scalars, tile, column, beside, metas, levels, cols):
+    find_transforms(num_y, (rows // BLK, float(cols), float(rows)), block_c, *ens, *metas, *refs[2 * num_y + 3 : -3])
+    mix_cells(levels, cols, block_c, mix_ref, x_ref, out_ref, *refs[-3:])
+
+
+def analyse_call(far, tile, column, beside, metas, levels, cols):
     num_y = len(column)
     _, members, rows = tile.shape
     slots = column[0].shape[1]
     count_r = rows // BLK
     vmem = pl.BlockSpec(memory_space=pltpu.VMEM)
     return pl.pallas_call(
-        functools.partial(analyse_kernel, num_y, (levels, cols, rows)),
-        in_specs=[pl.BlockSpec(memory_space=pltpu.SMEM)] + [vmem] * (2 * num_y + 3),
-        out_specs=vmem,
-        out_shape=pltpu.VMEM((members, levels * BLK, rows), bf16),
+        functools.partial(analyse_kernel, num_y, far, (levels, cols, rows)),
+        in_specs=[vmem] * (2 * num_y + 3),
+        out_specs=pl.BlockSpec(memory_space=pl.ANY),
+        out_shape=jax.ShapeDtypeStruct((members, levels * BLK, rows), bf16),
         scratch_shapes=[
             pltpu.VMEM((members, count_r * members), bf16),
             pltpu.VMEM((3 * count_r * members, 2 * slots), bf16),
             pltpu.VMEM((count_r, members, 4 * members), f32),
             pltpu.VMEM((count_r, 3, members, 2 * members), bf16),
             pltpu.VMEM((count_r, 3, members, 2 * members), bf16),
+            pltpu.VMEM((levels, members * PITCH, rows), f32),
+            pltpu.VMEM((levels, members, BLK, rows), bf16),
+            pltpu.SemaphoreType.DMA((levels,)),
         ],
         cost_estimate=pl.CostEstimate(flops=4 * 10**9, transcendentals=0, bytes_accessed=2 * 10**6),
         name="analyse",
-    )(scalars, *on_chip(tile, *column, *beside, *metas))
+    )(*on_chip(tile, *column, *beside, *metas))
 
 
 def pack_kernel(state_ref, out_ref, held_ref, in_sems, out_sems):
@@ -359,41 +371,44 @@
     def swap_y(value, first):
         return lax.ppermute(value, "gy", swap_pairs(n_y, first))
 
+    def swap_xy(value, first_x, first_y):
+        pairs = [
+            (sx * n_y + sy, dx * n_y + dy)
+            for sx, dx in swap_pairs(n_x, first_x)
+            for sy, dy in swap_pairs(n_y, first_y)
+        ]
+        return lax.ppermute(value, ("mem", "gy"), pairs)
+
     y_steps = [first for first in (0, 1) if swap_pairs(n_y, first)]
 
     live = jnp.arange(slots, dtype=jnp.int32) < obs_count[0, 0]
     weight = jnp.where(live, 1.0 / obs_var[0, 0], 0.0)
     col_pos = (obs_slots // rows % cols).astype(f32)
     row_pos = (obs_slots % rows).astype(f32)
-    blank = jnp.zeros((META - 4, slots), f32)
-    meta = jnp.concatenate([jnp.stack([obs_value[0, 0], weight, col_pos, row_pos]), blank], axis=0)
+    reach = jnp.broadcast_to(radius[0, 0].astype(f32), (slots,))
+    blank = jnp.zeros((META - 5, slots), f32)
+    meta = jnp.concatenate([jnp.stack([obs_value[0, 0], weight, col_pos, row_pos, reach]), blank], axis=0)
     meta_column = jnp.stack([meta] + [swap_y(meta, first) for first in y_steps])
     near_meta = swap_x(meta_column, 0)
     far_meta = swap_x(meta_column, 1)
-    odd_x = lax.axis_index("mem") & 1
-    odd_y = lax.axis_index("gy") & 1
-    scalars = [
-        jnp.stack([block_c, 2 * block_c - 1, odd_y, radius[0, 0]]).astype(jnp.int32) for block_c in (1 - odd_x, odd_x)
-    ]
-
     tile = lax.all_to_all(pack_call(state, n_x, cols), "mem", split_axis=0, concat_axis=0, tiled=True)
-    tile, meta_column, near_meta, scalars = lax.optimization_barrier((tile, meta_column, near_meta, scalars))
+    tile, meta_column, near_meta = lax.optimization_barrier((tile, meta_column, near_meta))
     tile = tile.reshape(members, levels * cols, rows)
 
     own = gather_call(tile, obs_slots)
-    column = [own] + [swap_y(own, first) for first in y_steps]
+    column = [own] + [swap_y(own, step) for step in y_steps]
+    near = [swap_x(own, 0)] + [swap_xy(own, 0, step) for step in y_steps]
     far_own = swap_x(own, 1)
     tile = turn_call(tile)
-    near = [swap_x(ens, 0) for ens in column]
 
     def send_back(analysed):
         analysed = analysed.reshape(n_x, held, levels, BLK, rows)
         return lax.all_to_all(analysed, "mem", split_axis=0, concat_axis=0, tiled=True)
 
-    analysed = analyse_call(scalars[0], tile, column, near, (meta_column, near_meta), levels, cols)
+    analysed = analyse_call(False, tile, column, near, (meta_column, near_meta), levels, cols)
     first = send_back(analysed)
     far = [far_own] + [swap_y(far_own, step) for step in y_steps]
-    analysed = analyse_call(scalars[1], tile, column, far, (meta_column, far_meta), levels, cols)
+    analysed = analyse_call(True, tile, column, far, (meta_column, far_meta), levels, cols)
     second = send_back(analysed)
     whole = unpack_call(1, first)
     return unpack_call(0, second, whole)

time: 103 us -> 100 us (0.971)
  Pallas kernels: 21.3 us -> 19.1 us
    ppermute x3, starting transfers between devices: 3.84 us -> 1.82 us  [swap_y(): return lax.ppermute(value, 'gy', swap_pairs(n_y, first))]
    pallas_call x2, Pallas kernels: 15.4 us -> 13.9 us  [analyse_call(): pl.pallas_call(functools.partial(analyse_kernel, num_y, far, (levels, col...]
    ppermute x5 -> x4, waiting for transfers between devices: 4.33 us -> 4.66 us  [swap_x(): return lax.ppermute(value, 'mem', swap_pairs(n_x, first))]
    ppermute x5 -> x4, starting transfers between devices: 9.02 us -> 8.97 us  [swap_x(): return lax.ppermute(value, 'mem', swap_pairs(n_x, first))]
  transfers between devices with their start and end apart: 11 -> 11, of which waited for: 8 -> 8; matrix products, arithmetic and copies ran while one was open for 1% -> 0% of each run, Pallas kernels for 9% -> 8%
where the time goes in v3:
time: 100 us; the launch traced here: 99.4 us
  starting transfers between devices  40.2 us (40%)
  waiting for transfers between devices  36.4 us (36%)
  Pallas kernels  19.1 us (19%)
  local copies, waits for them, and re-layouts  2.04 us (2%)
  between operations  1.58 us (2%)
    all_to_all x2, starting transfers between devices, send_back(): lax.all_to_all(analysed, 'mem', split_axis=0, concat_axis=0, tiled=True)  21.1 us
    all_to_all x1, waiting for transfers between devices, local(): lax.all_to_all(pack_call(state, n_x, cols), 'mem', split_axis=0, concat_a...  15.1 us
    pallas_call x2, Pallas kernels, analyse_call(): pl.pallas_call(functools.partial(analyse_kernel, num_y, far, (levels, col...  13.9 us
    all_to_all x2, waiting for transfers between devices, send_back(): lax.all_to_all(analysed, 'mem', split_axis=0, concat_axis=0, tiled=True)  13.1 us
    ppermute x4, starting transfers between devices, swap_x(): return lax.ppermute(value, 'mem', swap_pairs(n_x, first))  8.97 us
    all_to_all x1, starting transfers between devices, local(): lax.all_to_all(pack_call(state, n_x, cols), 'mem', split_axis=0, concat_a...  7.32 us
    ppermute x4, waiting for transfers between devices, swap_x(): return lax.ppermute(value, 'mem', swap_pairs(n_x, first))  4.66 us
    ppermute x3, waiting for transfers between devices, swap_y(): return lax.ppermute(value, 'gy', swap_pairs(n_y, first))  2.61 us
  transfers between devices with their start and end apart: 11, of which 8 were waited for; matrix products, arithmetic and copies ran while one was open for 0% of the time, Pallas kernels for 8%

profile of v3, /device:TPU:1, one launch (start us, length us, event | category | flops | bytes accessed | tf_op | source)
XLA Modules:
  0.0 99.4 jit_solution(7550093629771506449)
XLA Ops:
  0.0 2.2 %pack.1 = bf16[16,4,2,32,128]{4,3,2,1,0:T(8,128)(2,1)} custom-call(bf16[4,2,512,128]{3,2,1,0:T(8,128)(2,1)} %state_ref.1), custom_call_target="tpu_custom_call" | custom-call | tf_op jit(solution)/shard_map/pack/pallas_call | solution.py:313
  2.2 7.3 %all-to-all-start = ((bf16[16,4,2,32,128]{4,3,2,1,0:T(8,128)(2,1)}), bf16[16,4,2,32,128]{4,3,2,1,0:T(8,128)(2,1)S(1)}, u32[]{:S(2)}, u32[]{:S(2)}) async-start(bf16[16,4,2,32,128]{4,3,2,1,0:T(8,128)(2,1)} %pack.1), calls=%async_computation | async-start | bytes 2097152 | tf_op jit(solution)/shard_map/all_to_all | solution.py:394
  10.8 0.0 copy-start.2
  10.8 0.7 copy-done.2
  11.5 0.0 copy-start
  11.5 0.7 copy-done
  12.2 0.0 copy-start.1
  12.2 0.7 copy-done.1
  12.9 1.3 %collective-permute-start = (f32[8,256]{1,0:T(8,128)S(1)}, f32[8,256]{1,0:T(8,128)S(1)}, u32[]{:S(2)}, u32[]{:S(2)}) collective-permute-start(f32[8,256]{1,0:T(8,128)S(1)} %concatenate.3), channel_id=1, source_target_pairs={{0,1},{1,0},{2,3},{3,2},{4,5},{5,4},{6,7},{7,6},{8,9},{9,8},{10,11... | collective-permute-start | bytes 24584 | tf_op jit(solution)/shard_map/ppermute | solution.py:372
  14.2 1.6 %collective-permute-done = f32[8,256]{1,0:T(8,128)S(1)} collective-permute-done((f32[8,256]{1,0:T(8,128)S(1)}, f32[8,256]{1,0:T(8,128)S(1)}, u32[]{:S(2)}, u32[]{:S(2)}) %collective-permute-start) | collective-permute-done | bytes 8224 | tf_op jit(solution)/shard_map/ppermute | solution.py:372
  15.8 1.0 collective-permute-start.1
  16.7 0.8 collective-permute-done.1.refs_5_
  17.6 15.1 %all-to-all-done = bf16[16,4,2,32,128]{4,3,2,1,0:T(8,128)(2,1)S(1)} async-done(((bf16[16,4,2,32,128]{4,3,2,1,0:T(8,128)(2,1)}), bf16[16,4,2,32,128]{4,3,2,1,0:T(8,128)(2,1)S(1)}, u32[]{:S(2)}, u32[]{:S(2)}) %all-to-all-start) | async-done | bytes 1048608 | tf_op jit(solution)/shard_map/all_to_all | solution.py:394
  32.7 0.7 gather.1.refs_0_
  33.4 1.0 collective-permute-start.7
  34.4 0.7 collective-permute-start.6
  35.1 0.2 collective-permute-start.2
  35.3 0.5 turn.1.x_ref
  35.9 0.9 collective-permute-done.7.refs_3_
  36.8 0.0 collective-permute-done.6.refs_2_
  36.8 1.1 %collective-permute-done.2.refs_1_ = bf16[64,256]{1,0:T(8,128)(2,1)S(1)} collective-permute-done((bf16[64,256]{1,0:T(8,128)(2,1)S(1)}, bf16[64,256]{1,0:T(8,128)(2,1)S(1)}, u32[]{:S(2)}, u32[]{:S(2)}) %collective-permute-start.2) | collective-permute-done | bytes 32800 | tf_op jit(solution)/shard_map/ppermute | solution.py:372
  37.8 7.0 %analyse.3 = bf16[64,32,128]{2,1,0:T(8,128)(2,1)} custom-call(bf16[64,64,128]{2,1,0:T(8,128)(2,1)S(1)} %turn.1.x_ref, bf16[64,256]{1,0:T(8,128)(2,1)S(1)} %gather.1.refs_0_, bf16[64,256]{1,0:T(8,128)(2,1)S(1)} %collective-permute-done.2.refs_1_, bf16[64,256]{1,0:T(8,128)(2,1)S(1)} %collective-permute-done.6.refs_2_, ...), custom_call_target="tpu_custom_call" | custom-call | flops 4000000000 | bytes 2000000 | tf_op jit(solution)/shard_map/analyse/pallas_call | solution.py:274
  44.8 7.7 %all-to-all-start.2 = ((bf16[16,4,2,16,128]{4,3,2,1,0:T(8,128)(2,1)}), bf16[16,4,2,16,128]{4,3,2,1,0:T(8,128)(2,1)S(1)}, u32[]{:S(2)}, u32[]{:S(2)}) async-start(bf16[16,4,2,16,128]{4,3,2,1,0:T(8,128)(2,1)} %bitcast.18), calls=%async_computation.2 | async-start | bytes 1048576 | tf_op jit(solution)/shard_map/all_to_all | solution.py:406
  52.5 3.5 %collective-permute-start.3 = (bf16[64,256]{1,0:T(8,128)(2,1)S(1)}, bf16[64,256]{1,0:T(8,128)(2,1)S(1)}, u32[]{:S(2)}, u32[]{:S(2)}) collective-permute-start(bf16[64,256]{1,0:T(8,128)(2,1)S(1)} %gather.1.refs_0_), channel_id=1, source_target_pairs={{2,4},{4,2},{6,8},{8,6},{10,12},{12,10},{14,16},{16,14},{18,20},{2... | collective-permute-start | bytes 98312 | tf_op jit(solution)/shard_map/ppermute | solution.py:369
  56.0 2.2 %collective-permute-done.3.refs_2_ = bf16[64,256]{1,0:T(8,128)(2,1)S(1)} collective-permute-done((bf16[64,256]{1,0:T(8,128)(2,1)S(1)}, bf16[64,256]{1,0:T(8,128)(2,1)S(1)}, u32[]{:S(2)}, u32[]{:S(2)}) %collective-permute-start.3) | collective-permute-done | bytes 32800 | tf_op jit(solution)/shard_map/ppermute | solution.py:369
  58.2 0.3 collective-permute-start.4
  58.5 3.8 %collective-permute-start.5 = (f32[2,8,256]{2,1,0:T(8,128)S(1)}, f32[2,8,256]{2,1,0:T(8,128)S(1)}, u32[]{:S(2)}, u32[]{:S(2)}) collective-permute-start(f32[2,8,256]{2,1,0:T(8,128)S(1)} %pad_maximum_fusion.refs_4_), channel_id=1, source_target_pairs={{2,4},{4,2},{6,8},{8,6},{10,12},{12,10},{14,16},{16,14},{18,20},{2... | collective-permute-start | bytes 49160 | tf_op jit(solution)/shard_map/ppermute | solution.py:369
  62.3 1.6 %collective-permute-done.5.refs_5_ = f32[2,8,256]{2,1,0:T(8,128)S(1)} collective-permute-done((f32[2,8,256]{2,1,0:T(8,128)S(1)}, f32[2,8,256]{2,1,0:T(8,128)S(1)}, u32[]{:S(2)}, u32[]{:S(2)}) %collective-permute-start.5) | collective-permute-done | bytes 16416 | tf_op jit(solution)/shard_map/ppermute | solution.py:369
  63.9 0.0 collective-permute-done.4.refs_3_
  63.9 7.0 %analyse.2 = bf16[64,32,128]{2,1,0:T(8,128)(2,1)} custom-call(bf16[64,64,128]{2,1,0:T(8,128)(2,1)S(1)} %turn.1.x_ref, bf16[64,256]{1,0:T(8,128)(2,1)S(1)} %gather.1.refs_0_, bf16[64,256]{1,0:T(8,128)(2,1)S(1)} %collective-permute-done.2.refs_1_, bf16[64,256]{1,0:T(8,128)(2,1)S(1)} %collective-permute-done.3.refs_2_, ...), custom_call_target="tpu_custom_call" | custom-call | flops 4000000000 | bytes 2000000 | tf_op jit(solution)/shard_map/analyse/pallas_call | solution.py:274
  70.9 0.0 all-to-all-done.2.half_ref
  70.9 13.4 %all-to-all-start.1 = ((bf16[16,4,2,16,128]{4,3,2,1,0:T(8,128)(2,1)}), bf16[16,4,2,16,128]{4,3,2,1,0:T(8,128)(2,1)S(1)}, u32[]{:S(2)}, u32[]{:S(2)}) async-start(bf16[16,4,2,16,128]{4,3,2,1,0:T(8,128)(2,1)} %bitcast.19), calls=%async_computation.1 | async-start | bytes 1048576 | tf_op jit(solution)/shard_map/all_to_all | solution.py:406
  84.3 0.9 unpack.2.refs_0_
  85.2 13.1 %all-to-all-done.1.half_ref = bf16[16,4,2,16,128]{4,3,2,1,0:T(8,128)(2,1)S(1)} async-done(((bf16[16,4,2,16,128]{4,3,2,1,0:T(8,128)(2,1)}), bf16[16,4,2,16,128]{4,3,2,1,0:T(8,128)(2,1)S(1)}, u32[]{:S(2)}, u32[]{:S(2)}) %all-to-all-start.1) | async-done | bytes 524320 | tf_op jit(solution)/shard_map/all_to_all | solution.py:406
  98.3 0.9 unpack.3
  (7 shorter events, 0.1 us)
Async XLA Ops:
  2.2 30.5 %all-to-all-start = ((bf16[16,4,2,32,128]{4,3,2,1,0:T(8,128)(2,1)}), bf16[16,4,2,32,128]{4,3,2,1,0:T(8,128)(2,1)S(1)}, u32[]{:S(2)}, u32[]{:S(2)}) async-start(bf16[16,4,2,32,128]{4,3,2,1,0:T(8,128)(2,1)} %pack.1), calls=%async_computation | async-start | bytes 2097152 | tf_op jit(solution)/shard_map/all_to_all | solution.py:394
  10.8 0.7 copy-start.2
  11.5 0.7 copy-start
  12.2 0.7 copy-start.1
  12.9 2.9 %collective-permute-start = (f32[8,256]{1,0:T(8,128)S(1)}, f32[8,256]{1,0:T(8,128)S(1)}, u32[]{:S(2)}, u32[]{:S(2)}) collective-permute-start(f32[8,256]{1,0:T(8,128)S(1)} %concatenate.3), channel_id=1, source_target_pairs={{0,1},{1,0},{2,3},{3,2},{4,5},{5,4},{6,7},{7,6},{8,9},{9,8},{10,11... | collective-permute-start | bytes 24584 | tf_op jit(solution)/shard_map/ppermute | solution.py:372
  15.8 1.8 %collective-permute-start.1 = (f32[2,8,256]{2,1,0:T(8,128)S(1)}, f32[2,8,256]{2,1,0:T(8,128)S(1)}, u32[]{:S(2)}, u32[]{:S(2)}) collective-permute-start(f32[2,8,256]{2,1,0:T(8,128)S(1)} %pad_maximum_fusion.refs_4_), channel_id=1, source_target_pairs={{0,2},{2,0},{4,6},{6,4},{8,10},{10,8},{12,14},{14,12},{16,18},{18,... | collective-permute-start | bytes 49160 | tf_op jit(solution)/shard_map/ppermute | solution.py:369
  33.4 3.4 %collective-permute-start.7 = (bf16[64,256]{1,0:T(8,128)(2,1)S(1)}, bf16[64,256]{1,0:T(8,128)(2,1)S(1)}, u32[]{:S(2)}, u32[]{:S(2)}) collective-permute-start(bf16[64,256]{1,0:T(8,128)(2,1)S(1)} %gather.1.refs_0_), channel_id=1, source_target_pairs={{0,3},{1,2},{2,1},{3,0},{4,7},{5,6},{6,5},{7,4},{8,11},{9,10},{10,... | collective-permute-start | bytes 98312 | tf_op jit(solution)/shard_map/ppermute | solution.py:380
  34.4 2.4 %collective-permute-start.6 = (bf16[64,256]{1,0:T(8,128)(2,1)S(1)}, bf16[64,256]{1,0:T(8,128)(2,1)S(1)}, u32[]{:S(2)}, u32[]{:S(2)}) collective-permute-start(bf16[64,256]{1,0:T(8,128)(2,1)S(1)} %gather.1.refs_0_), channel_id=1, source_target_pairs={{0,2},{2,0},{4,6},{6,4},{8,10},{10,8},{12,14},{14,12},{16,18},{18,... | collective-permute-start | bytes 98312 | tf_op jit(solution)/shard_map/ppermute | solution.py:369
  35.1 2.8 %collective-permute-start.2 = (bf16[64,256]{1,0:T(8,128)(2,1)S(1)}, bf16[64,256]{1,0:T(8,128)(2,1)S(1)}, u32[]{:S(2)}, u32[]{:S(2)}) collective-permute-start(bf16[64,256]{1,0:T(8,128)(2,1)S(1)} %gather.1.refs_0_), channel_id=1, source_target_pairs={{0,1},{1,0},{2,3},{3,2},{4,5},{5,4},{6,7},{7,6},{8,9},{9,8},{10,11... | collective-permute-start | bytes 98312 | tf_op jit(solution)/shard_map/ppermute | solution.py:372
  44.8 26.1 %all-to-all-start.2 = ((bf16[16,4,2,16,128]{4,3,2,1,0:T(8,128)(2,1)}), bf16[16,4,2,16,128]{4,3,2,1,0:T(8,128)(2,1)S(1)}, u32[]{:S(2)}, u32[]{:S(2)}) async-start(bf16[16,4,2,16,128]{4,3,2,1,0:T(8,128)(2,1)} %bitcast.18), calls=%async_computation.2 | async-start | bytes 1048576 | tf_op jit(solution)/shard_map/all_to_all | solution.py:406
  52.5 5.8 %collective-permute-start.3 = (bf16[64,256]{1,0:T(8,128)(2,1)S(1)}, bf16[64,256]{1,0:T(8,128)(2,1)S(1)}, u32[]{:S(2)}, u32[]{:S(2)}) collective-permute-start(bf16[64,256]{1,0:T(8,128)(2,1)S(1)} %gather.1.refs_0_), channel_id=1, source_target_pairs={{2,4},{4,2},{6,8},{8,6},{10,12},{12,10},{14,16},{16,14},{18,20},{2... | collective-permute-start | bytes 98312 | tf_op jit(solution)/shard_map/ppermute | solution.py:369
  58.2 5.7 %collective-permute-start.4 = (bf16[64,256]{1,0:T(8,128)(2,1)S(1)}, bf16[64,256]{1,0:T(8,128)(2,1)S(1)}, u32[]{:S(2)}, u32[]{:S(2)}) collective-permute-start(bf16[64,256]{1,0:T(8,128)(2,1)S(1)} %collective-permute-done.3.refs_2_), channel_id=1, source_target_pairs={{0,1},{1,0},{2,3},{3,2},{4,5},{5,4},{6,7},{7,6},{8,9},{9,8},{10,11... | collective-permute-start | bytes 98312 | tf_op jit(solution)/shard_map/ppermute | solution.py:372
  58.5 5.4 %collective-permute-start.5 = (f32[2,8,256]{2,1,0:T(8,128)S(1)}, f32[2,8,256]{2,1,0:T(8,128)S(1)}, u32[]{:S(2)}, u32[]{:S(2)}) collective-permute-start(f32[2,8,256]{2,1,0:T(8,128)S(1)} %pad_maximum_fusion.refs_4_), channel_id=1, source_target_pairs={{2,4},{4,2},{6,8},{8,6},{10,12},{12,10},{14,16},{16,14},{18,20},{2... | collective-permute-start | bytes 49160 | tf_op jit(solution)/shard_map/ppermute | solution.py:369
  70.9 27.4 %all-to-all-start.1 = ((bf16[16,4,2,16,128]{4,3,2,1,0:T(8,128)(2,1)}), bf16[16,4,2,16,128]{4,3,2,1,0:T(8,128)(2,1)S(1)}, u32[]{:S(2)}, u32[]{:S(2)}) async-start(bf16[16,4,2,16,128]{4,3,2,1,0:T(8,128)(2,1)} %bitcast.19), calls=%async_computation.1 | async-start | bytes 1048576 | tf_op jit(solution)/shard_map/all_to_all | solution.py:406
